TPU v7x, 32 devices: a whole 2x2x4 slice. The times are simulated.
32 devices in a mesh: wide: 8 (over y, x, core), narrow: 4 (over z).
Axes of the slice: x: 2, y: 2, z: 4, core: 2. Of those that a mesh axis runs over, the one named last changes fastest.
Arguments:
- latent: float32 [2, 64, 256, 512], P(None, 'wide', 'narrow'), may hold values from -6 to 6
- context: bfloat16 [2, 32, 128, 256], P(None, 'wide', 'narrow'), may hold values from -6 to 6
- conv_weight: bfloat16 [3, 3, 256, 512], replicated, may hold values from -0.125 to 0.125
- window_qkv: bfloat16 [512, 1536], replicated, may hold values from -0.25 to 0.25
- window_out: bfloat16 [512, 512], replicated, may hold values from -0.25 to 0.25
- window_bias: float32 [16, 15, 15], replicated, may hold values from -9 to 320
- grid_qkv: bfloat16 [512, 1536], replicated, may hold values from -0.25 to 0.25
- grid_out: bfloat16 [512, 512], replicated, may hold values from -0.25 to 0.25
- grid_bias: float32 [16, 15, 15], replicated, may hold values from -9 to 320
- mlp_gain: float32 [512], replicated, may hold values from 0.1 to 1.9
- mlp_in: bfloat16 [512, 2048], replicated, may hold values from -0.25 to 0.25
- mlp_out: bfloat16 [2048, 512], replicated, may hold values from -0.125 to 0.125
Outputs:
- forecast: float32 [2, 64, 256, 512], P(None, 'wide', 'narrow')
All inputs are finite; a program needn't handle non-finite values.
Results may differ from a plain program's by a relative error of at most 0.0055.
Values may be sent and summed in bfloat16 or wider, within the bound.
No kernel may reach another device: no remote copies, remote signals or barrier semaphores. Data moves between devices by JAX's collectives and lax.ppermute only.
A program may use at most 128 MiB of HBM per device.

v0:
```python
import functools

import jax
import jax.numpy as jnp
import numpy as np
from jax import lax
from jax.experimental import pallas as pl
from jax.experimental.pallas import tpu as pltpu
from jax.sharding import PartitionSpec as P

HEAD = 32
WIN = 8
NORM_EPS = 1e-05
LANES = 128
JOINT = ("wide", "narrow")


def neighbours(block, axis, dim, width):
    count = lax.axis_size(axis)
    forward = [(i, i + 1) for i in range(count - 1)]
    backward = [(target, source) for source, target in forward]
    low = lax.ppermute(
        lax.slice_in_dim(block, block.shape[dim] - width, None, axis=dim), axis, forward
    )
    high = lax.ppermute(lax.slice_in_dim(block, 0, width, axis=dim), axis, backward)
    return low, high


def shifted_bias(tables):
    side = WIN
    rows = jnp.stack([tables[:, :, side - 1 - c : 2 * side - 1 - c] for c in range(side)], axis=1)
    flat = rows.reshape(tables.shape[0], side, (2 * side - 1) * side)
    return jnp.pad(flat, ((0, 0), (0, 0), (0, LANES - flat.shape[2])))


def fill_bias(shifted_ref, table_ref):
    heads = shifted_ref.shape[0]
    low_half = lax.broadcasted_iota(jnp.int32, (WIN, LANES), 1) < WIN * WIN
    for pair in range(heads // 2):
        even = shifted_ref[2 * pair]
        odd = shifted_ref[2 * pair + 1]
        for key_row in range(WIN):
            start = WIN * (WIN - 1 - key_row)
            even_part = pltpu.roll(even, (LANES - start) % LANES, 1)
            odd_part = pltpu.roll(odd, (LANES - start + WIN * WIN) % LANES, 1)
            table_ref[key_row * WIN : (key_row + 1) * WIN, pair * LANES : (pair + 1) * LANES] = (
                jnp.where(low_half, even_part, odd_part)
            )


def layer_norm(values):
    center = values - jnp.mean(values, axis=-1, keepdims=True)
    spread = jnp.mean(center * center, axis=-1, keepdims=True)
    return center * lax.rsqrt(spread + NORM_EPS)


def attend(qk_ref, vt_ref, bias_ref, row_start, lane_start, half, channels):
    members = WIN * WIN
    lane_head = lax.broadcasted_iota(jnp.int32, (members, LANES), 1) // HEAD
    low_half = lax.broadcasted_iota(jnp.int32, (HEAD, LANES), 1) < members
    per = LANES // HEAD
    pieces = []
    for block in range(channels // LANES):
        queries = qk_ref[pl.ds(row_start, members), block * LANES : (block + 1) * LANES]
        keys = qk_ref[
            pl.ds(row_start, members),
            channels + block * LANES : channels + (block + 1) * LANES,
        ]
        zero = jnp.zeros_like(queries)
        spread = jnp.concatenate(
            [jnp.where(lane_head == h, queries, zero) for h in range(per)], axis=0
        )
        scores = lax.dot_general(
            keys, spread, (((1,), (1,)), ((), ())), preferred_element_type=jnp.float32
        )
        wide = per * members
        scores = scores * HEAD ** (-0.5) + bias_ref[:, block * wide : (block + 1) * wide]
        lifted = jnp.exp(scores - jnp.max(scores, axis=0, keepdims=True))
        weights = lifted * (1.0 / jnp.sum(lifted, axis=0, keepdims=True))
        weights = weights.astype(jnp.bfloat16)
        for pair in range(per // 2):
            first = block * LANES + pair * 2 * HEAD
            values = vt_ref[first : first + 2 * HEAD, pl.ds(lane_start, LANES)]
            values = values[:, half * members : (half + 1) * members]
            mixed = jnp.dot(
                values,
                weights[:, pair * LANES : (pair + 1) * LANES],
                preferred_element_type=jnp.float32,
            )
            pieces.append(jnp.where(low_half, mixed[:HEAD], mixed[HEAD:]))
    turned = jnp.concatenate(pieces, axis=0).T
    return jnp.concatenate([turned[:members], turned[members:]], axis=1)


def out_copies(weight_ref, buffer_ref, sem):
    pairs = weight_ref.shape[0] // (2 * HEAD)
    return [
        pltpu.make_async_copy(
            weight_ref.at[pl.ds((2 * pair + parity) * HEAD, HEAD)],
            buffer_ref.at[pl.ds((parity * pairs + pair) * HEAD, HEAD)],
            sem,
        )
        for parity in range(2)
        for pair in range(pairs)
    ]


def window_kernel(
    place_ref,
    latent_ref,
    context_ref,
    low_ref,
    high_ref,
    left_ref,
    right_ref,
    lift_ref,
    shifted_ref,
    conv_hbm,
    qkv_hbm,
    vt_hbm,
    out_hbm,
    residual_ref,
    normed_ref,
    conv_w,
    qk_w,
    vt_w,
    out_w,
    wide_s,
    taps_s,
    features_s,
    normed_s,
    qk_s,
    vt_s,
    heads_s,
    bias_s,
    sems,
    *,
    stride,
):
    rows, cols, channels = latent_ref.shape
    half_rows, half_cols, coarse = context_ref.shape
    members = WIN * WIN
    windows = cols // WIN
    copies = [
        pltpu.make_async_copy(conv_hbm, conv_w, sems.at[0]),
        pltpu.make_async_copy(qkv_hbm.at[:, pl.ds(0, 2 * channels)], qk_w, sems.at[1]),
        pltpu.make_async_copy(vt_hbm, vt_w, sems.at[2]),
    ]
    placed = out_copies(out_hbm, out_w, sems.at[3])
    for copy in copies + placed:
        copy.start()
    span = half_rows + 2
    wide_s[...] = jnp.zeros_like(wide_s)
    for row in range(half_rows + 4):
        base = row * stride
        if row < 2:
            middle = low_ref[row]
        elif row < half_rows + 2:
            middle = context_ref[row - 2]
        else:
            middle = high_ref[row - half_rows - 2]
        wide_s[base : base + 2] = left_ref[row].astype(jnp.float32)
        wide_s[base + 2 : base + 2 + half_cols] = middle.astype(jnp.float32)
        wide_s[base + 2 + half_cols : base + 4 + half_cols] = right_ref[row].astype(jnp.float32)
    tall = (half_rows + 4) * stride
    for shift in range(3):
        taps_s[:, shift * coarse : (shift + 1) * coarse] = wide_s[shift : shift + tall].astype(
            jnp.bfloat16
        )
    fill_bias(shifted_ref, bias_s)
    copies[0].wait()
    total = jnp.zeros((span * stride, channels), jnp.float32)
    for shift in range(3):
        total = total + jnp.dot(
            taps_s[shift * stride : (shift + span) * stride],
            conv_w[shift],
            preferred_element_type=jnp.float32,
        )
    flat = lax.broadcasted_iota(jnp.int32, (span * stride, 1), 0)
    row_place = flat // stride + place_ref[0]
    col_place = flat % stride + place_ref[1]
    inside = (row_place >= 0) & (row_place < place_ref[2])
    inside = inside & (col_place >= 0) & (col_place < place_ref[3])
    inside = inside & (flat % stride < half_cols + 2)
    features_s[...] = jnp.where(inside, total, 0.0).astype(jnp.bfloat16)

    for window in range(windows):
        cells = latent_ref[:, window * WIN : (window + 1) * WIN, :].reshape(members, channels)
        lifted = jnp.dot(lift_ref[window], features_s[...], preferred_element_type=jnp.float32)
        residual = cells + lifted
        residual_ref[window] = residual
        normed_s[window * members : (window + 1) * members] = layer_norm(residual).astype(
            jnp.bfloat16
        )

    copies[1].wait()
    for block in range(4):
        part = slice(block * channels // 2, (block + 1) * channels // 2)
        qk_s[:, part] = jnp.dot(
            normed_s[...], qk_w[:, part], preferred_element_type=jnp.float32
        ).astype(jnp.bfloat16)
    copies[2].wait()
    vt_s[...] = lax.dot_general(
        vt_w[...], normed_s[...], (((1,), (1,)), ((), ())), preferred_element_type=jnp.float32
    ).astype(jnp.bfloat16)

    def two_windows(step, carry):
        for half in range(2):
            row_start = pl.multiple_of((2 * step + half) * members, members)
            heads = attend(
                qk_s, vt_s, bias_s, row_start, pl.multiple_of(step * LANES, LANES), half, channels
            )
            heads_s[pl.ds(row_start, members)] = heads.astype(jnp.bfloat16)
        return carry

    lax.fori_loop(0, windows // 2, two_windows, 0)
    for copy in placed:
        copy.wait()
    narrow = normed_ref.shape[1]
    for window in range(windows):
        part = slice(window * members, (window + 1) * members)
        residual = residual_ref[window] + jnp.dot(
            heads_s[part], out_w[...], preferred_element_type=jnp.float32
        )
        residual_ref[window] = residual
        normed = layer_norm(residual).astype(jnp.bfloat16).reshape(rows, WIN, channels)
        normed_ref[:, window % narrow, window // narrow] = normed


def grid_kernel(
    cells_ref,
    shifted_ref,
    qkv_hbm,
    vt_hbm,
    heads_ref,
    qk_w,
    vt_w,
    spread_s,
    normed_s,
    qk_s,
    vt_s,
    bias_s,
    sems,
):
    members, groups, channels = cells_ref.shape
    copies = [
        pltpu.make_async_copy(qkv_hbm.at[:, pl.ds(0, 2 * channels)], qk_w, sems.at[0]),
        pltpu.make_async_copy(vt_hbm, vt_w, sems.at[1]),
    ]
    for copy in copies:
        copy.start()
    fill_bias(shifted_ref, bias_s)
    spread_s[...] = cells_ref[...].astype(jnp.float32)
    for group in range(groups):
        normed_s[group * members : (group + 1) * members] = spread_s[:, group, :].astype(
            jnp.bfloat16
        )
    copies[0].wait()
    for block in range(4):
        part = slice(block * channels // 2, (block + 1) * channels // 2)
        qk_s[:, part] = jnp.dot(
            normed_s[...], qk_w[:, part], preferred_element_type=jnp.float32
        ).astype(jnp.bfloat16)
    copies[1].wait()
    vt_s[...] = lax.dot_general(
        vt_w[...], normed_s[...], (((1,), (1,)), ((), ())), preferred_element_type=jnp.float32
    ).astype(jnp.bfloat16)

    for step in range(groups // 2):
        for half in range(2):
            group = 2 * step + half
            heads = attend(
                qk_s, vt_s, bias_s, group * members, step * LANES, half, channels
            )
            spread_s[:, group, :] = heads
    heads_ref[...] = spread_s[...].astype(jnp.bfloat16)


def mlp_kernel(
    residual_ref,
    heads_ref,
    gain_ref,
    out_hbm,
    first_hbm,
    second_hbm,
    result_ref,
    out_w,
    first_w,
    second_w,
    residual_s,
    normed_s,
    sems,
):
    windows, members, channels = residual_ref.shape
    rows, narrow = heads_ref.shape[:2]
    hidden = first_w.shape[1]
    placed = out_copies(out_hbm, out_w, sems.at[0])
    copies = [
        pltpu.make_async_copy(first_hbm, first_w, sems.at[1]),
        pltpu.make_async_copy(second_hbm, second_w, sems.at[2]),
    ]
    for copy in placed + copies:
        copy.start()
    for copy in placed:
        copy.wait()
    for window in range(windows):
        heads = heads_ref[:, window % narrow, window // narrow].reshape(members, channels)
        residual = residual_ref[window] + jnp.dot(
            heads, out_w[...], preferred_element_type=jnp.float32
        )
        part = slice(window * members, (window + 1) * members)
        residual_s[part] = residual
        normed_s[part] = (layer_norm(residual) * gain_ref[...]).astype(jnp.bfloat16)
    for copy in copies:
        copy.wait()
    step_size = channels // 2

    def one_block(step, carry):
        start = pl.multiple_of(step * step_size, step_size)
        inner = jnp.dot(
            normed_s[...], first_w[:, pl.ds(start, step_size)], preferred_element_type=jnp.float32
        )
        cubed = 0.7978845608028654 * (inner + 0.044715 * (inner * inner * inner))
        active = (0.5 * inner * (1.0 + jnp.tanh(cubed))).astype(jnp.bfloat16)
        residual_s[...] += jnp.dot(
            active, second_w[pl.ds(start, step_size)], preferred_element_type=jnp.float32
        )
        return carry

    lax.fori_loop(0, hidden // step_size, one_block, 0)
    for window in range(windows):
        result_ref[:, window * WIN : (window + 1) * WIN, :] = residual_s[
            window * members : (window + 1) * members
        ].reshape(rows, WIN, channels)


VMEM = pl.BlockSpec(memory_space=pltpu.MemorySpace.VMEM)
ANY = pl.BlockSpec(memory_space=pl.ANY)
SMEM = pl.BlockSpec(memory_space=pltpu.MemorySpace.SMEM)
PARAMS = dict(vmem_limit_bytes=48 * 1024 * 1024)


def lift_matrix(rows, cols, stride):
    def along(count):
        fine = np.arange(count)
        place = np.zeros((count, count // 2 + 2), np.float32)
        middle = fine // 2 + 1
        place[fine, middle] = 0.75
        place[fine, middle + np.where(fine % 2 == 0, -1, 1)] = 0.25
        return place

    by_row = along(rows)
    by_col = along(cols)
    by_col = np.pad(by_col, ((0, 0), (0, stride - by_col.shape[1])))
    both = by_row[:, None, :, None] * by_col[None, :, None, :]
    both = both.reshape(rows, cols // WIN, WIN, -1).transpose(1, 0, 2, 3)
    return jnp.asarray(both.reshape(cols // WIN, rows * WIN, -1), jnp.bfloat16)


def on_device(
    latent,
    context,
    conv_weight,
    window_qkv,
    window_out,
    window_bias,
    grid_qkv,
    grid_out,
    grid_bias,
    mlp_gain,
    mlp_in,
    mlp_out,
):
    samples, rows, cols, channels = latent.shape
    wide_count = lax.axis_size("wide")
    narrow = lax.axis_size("narrow")
    half_rows, half_cols, coarse = context.shape[1:]
    hidden = mlp_in.shape[1]
    members = WIN * WIN
    windows = cols // WIN
    planes = WIN // narrow
    split = wide_count // WIN
    assert rows == WIN and planes * narrow == WIN and split * WIN == wide_count
    assert windows == planes * narrow and WIN % split == 0
    stride = -(-(half_cols + 4) // 16) * 16

    low, high = neighbours(context, "wide", 1, 2)
    widened = jnp.concatenate([low, context, high], axis=1)
    left, right = neighbours(widened, "narrow", 2, 2)
    shifted = shifted_bias(jnp.concatenate([window_bias, grid_bias], axis=0))
    heads_count = window_bias.shape[0]
    window_shifted, grid_shifted = shifted[:heads_count], shifted[heads_count:]
    window_vt = window_qkv[:, 2 * channels :].T
    grid_vt = grid_qkv[:, 2 * channels :].T
    lift = lift_matrix(rows, cols, stride)
    conv_flat = conv_weight.reshape(3, 3 * coarse, channels)
    place = jnp.stack(
        [
            lax.axis_index("wide") * half_rows - 1,
            lax.axis_index("narrow") * half_cols - 1,
            jnp.int32(wide_count * half_rows),
            jnp.int32(narrow * half_cols),
        ]
    ).astype(jnp.int32)

    bf16, f32 = jnp.bfloat16, jnp.float32
    tokens = rows * cols
    span = half_rows + 2
    window_call = pl.pallas_call(
        functools.partial(window_kernel, stride=stride),
        out_shape=(
            jax.ShapeDtypeStruct((windows, members, channels), f32),
            jax.ShapeDtypeStruct((rows, narrow, planes, WIN, channels), bf16),
        ),
        in_specs=[SMEM] + [VMEM] * 8 + [ANY] * 4,
        out_specs=(VMEM, VMEM),
        scratch_shapes=[
            pltpu.VMEM((3, 3 * coarse, channels), bf16),
            pltpu.VMEM((channels, 2 * channels), bf16),
            pltpu.VMEM((channels, channels), bf16),
            pltpu.VMEM((channels, channels), bf16),
            pltpu.VMEM(((half_rows + 4) * stride + 16, coarse), f32),
            pltpu.VMEM(((half_rows + 4) * stride, 3 * coarse), bf16),
            pltpu.VMEM((span * stride, channels), bf16),
            pltpu.VMEM((tokens, channels), bf16),
            pltpu.VMEM((tokens, 2 * channels), bf16),
            pltpu.VMEM((channels, tokens), bf16),
            pltpu.VMEM((tokens, channels), bf16),
            pltpu.VMEM((members, heads_count * members), f32),
            pltpu.SemaphoreType.DMA((4,)),
        ],
        compiler_params=pltpu.CompilerParams(**PARAMS),
        name="window",
    )
    groups = WIN
    grid_call = pl.pallas_call(
        grid_kernel,
        out_shape=jax.ShapeDtypeStruct((members, groups, channels), bf16),
        in_specs=[VMEM] * 2 + [ANY] * 2,
        out_specs=VMEM,
        scratch_shapes=[
            pltpu.VMEM((channels, 2 * channels), bf16),
            pltpu.VMEM((channels, channels), bf16),
            pltpu.VMEM((members, groups, channels), f32),
            pltpu.VMEM((tokens, channels), bf16),
            pltpu.VMEM((tokens, 2 * channels), bf16),
            pltpu.VMEM((channels, tokens), bf16),
            pltpu.VMEM((members, heads_count * members), f32),
            pltpu.SemaphoreType.DMA((2,)),
        ],
        compiler_params=pltpu.CompilerParams(**PARAMS),
        name="grid",
    )
    mlp_call = pl.pallas_call(
        mlp_kernel,
        out_shape=jax.ShapeDtypeStruct((rows, cols, channels), f32),
        in_specs=[VMEM] * 3 + [ANY] * 3,
        out_specs=VMEM,
        scratch_shapes=[
            pltpu.VMEM((channels, channels), bf16),
            pltpu.VMEM((channels, hidden), bf16),
            pltpu.VMEM((hidden, channels), bf16),
            pltpu.VMEM((tokens, channels), f32),
            pltpu.VMEM((tokens, channels), bf16),
            pltpu.SemaphoreType.DMA((3,)),
        ],
        compiler_params=pltpu.CompilerParams(**PARAMS),
        name="mlp",
    )
    gain = mlp_gain.reshape(1, channels)

    def send(normed):
        pieces = normed.reshape(rows, narrow, planes, split, WIN // split, channels)
        pieces = pieces.transpose(0, 3, 1, 2, 4, 5)
        pieces = pieces.reshape(wide_count * narrow, planes, WIN // split, channels)
        received = lax.all_to_all(pieces, JOINT, split_axis=0, concat_axis=0, tiled=True)
        received = received.reshape(WIN, split, narrow, planes, WIN // split, channels)
        return received.transpose(0, 2, 3, 1, 4, 5).reshape(members, WIN, channels)

    def send_back(heads):
        pieces = heads.reshape(WIN, narrow, planes, split, WIN // split, channels)
        pieces = pieces.transpose(0, 3, 1, 2, 4, 5)
        pieces = pieces.reshape(wide_count * narrow, planes, WIN // split, channels)
        received = lax.all_to_all(pieces, JOINT, split_axis=0, concat_axis=0, tiled=True)
        received = received.reshape(rows, split, narrow, planes, WIN // split, channels)
        return received.transpose(0, 2, 3, 1, 4, 5).reshape(rows, narrow, planes, WIN, channels)

    residuals, cells = [], []
    for sample in range(samples):
        residual, normed = window_call(
            place,
            latent[sample],
            context[sample],
            low[sample],
            high[sample],
            left[sample],
            right[sample],
            lift,
            window_shifted,
            conv_flat,
            window_qkv,
            window_vt,
            window_out,
        )
        residuals.append(residual)
        cells.append(send(normed))
    returned = []
    for sample in range(samples):
        heads = grid_call(cells[sample], grid_shifted, grid_qkv, grid_vt)
        returned.append(send_back(heads))
    results = [
        mlp_call(residuals[sample], returned[sample], gain, grid_out, mlp_in, mlp_out)
        for sample in range(samples)
    ]
    return jnp.stack(results)


def solution(mesh):
    return jax.shard_map(
        on_device,
        mesh=mesh,
        in_specs=(
            P(None, "wide", "narrow", None),
            P(None, "wide", "narrow", None),
        )
        + (P(),) * 10,
        out_specs=P(None, "wide", "narrow", None),
        check_vma=False,
    )
```

profile of v0, /device:TPU:1, one launch (start us, length us, event | category | flops | bytes accessed | tf_op | source)
XLA Modules:
  0.0 143.8 jit_solution(8445976128039948283)
XLA Ops:
  0.0 1.5 %fusion.2 = (bf16[2,2,32,256]{3,2,1,0:T(8,128)(2,1)}, bf16[2,2,32,256]{3,2,1,0:T(8,128)(2,1)}) fusion(bf16[2,4,32,256]{3,2,1,0:T(8,128)(2,1)} %param.14), kind=kLoop, calls=%fused_computation.23 | loop fusion | bytes 262144 | tf_op jit(solution)/shard_map/slice | solution.py:25
  1.5 4.5 %collective-permute-start = (bf16[2,2,32,256]{3,2,1,0:T(8,128)(2,1)}, bf16[2,2,32,256]{3,2,1,0:T(8,128)(2,1)}, u32[]{:S(2)}, u32[]{:S(2)}) collective-permute-start(bf16[2,2,32,256]{3,2,1,0:T(8,128)(2,1)} %get-tuple-element.30), channel_id=1, source_target_pairs={{0,4},{4,8},{8,12},{12,16},{16,20},{20,24},{24,28},{1,5},{5,9},{9,... | collective-permute-start | bytes 196616 | tf_op jit(solution)/shard_map/ppermute | solution.py:22
  6.0 1.9 %collective-permute-start.1 = (bf16[2,2,32,256]{3,2,1,0:T(8,128)(2,1)}, bf16[2,2,32,256]{3,2,1,0:T(8,128)(2,1)}, u32[]{:S(2)}, u32[]{:S(2)}) collective-permute-start(bf16[2,2,32,256]{3,2,1,0:T(8,128)(2,1)} %get-tuple-element.29), channel_id=1, source_target_pairs={{4,0},{8,4},{12,8},{16,12},{20,16},{24,20},{28,24},{5,1},{9,5},{13... | collective-permute-start | bytes 196616 | tf_op jit(solution)/shard_map/ppermute | solution.py:25
  8.0 1.5 %slice_bitcast_fusion.3 = (bf16[4,32,256]{2,1,0:T(8,128)(2,1)}, bf16[4,32,256]{2,1,0:T(8,128)(2,1)}) fusion(bf16[2,4,32,256]{3,2,1,0:T(8,128)(2,1)} %param.14), kind=kLoop, calls=%fused_computation.6 | loop fusion | bytes 262144 | tf_op jit(solution)/shard_map/squeeze | solution.py:493
  11.3 1.3 fusion.1
  18.1 1.6 %slice_bitcast_fusion.1 = (f32[8,64,512]{2,1,0:T(8,128)}, f32[8,64,512]{2,1,0:T(8,128)}) fusion(f32[2,8,64,512]{3,2,1,0:T(8,128)S(1)} %copy-done.29), kind=kLoop, calls=%fused_computation.2 | loop fusion | bytes 4194304 | tf_op jit(solution)/shard_map/squeeze | solution.py:492
  24.2 4.0 %collective-permute-start.2 = (bf16[2,8,2,256]{3,2,1,0:T(2,128)(2,1)S(1)}, bf16[2,8,2,256]{3,2,1,0:T(2,128)(2,1)S(1)}, u32[]{:S(2)}, u32[]{:S(2)}) collective-permute-start(bf16[2,8,2,256]{3,2,1,0:T(2,128)(2,1)S(1)} %get-tuple-element.16), channel_id=1, source_target_pairs={{0,1},{1,2},{2,3},{4,5},{5,6},{6,7},{8,9},{9,10},{10,11},{12,13},{... | collective-permute-start | bytes 49160 | tf_op jit(solution)/shard_map/ppermute | solution.py:22
  28.2 1.4 slice_bitcast_fusion.6
  29.5 1.4 slice_bitcast_fusion.7
  33.9 11.9 %window.2 = (f32[8,64,512]{2,1,0:T(8,128)S(1)}, bf16[8,4,2,8,512]{4,3,2,1,0:T(8,128)(2,1)S(1)}) custom-call(s32[4]{0:T(128)S(1)} %pad_add_fusion.place_ref, f32[8,64,512]{2,1,0:T(8,128)S(1)} %copy-done.5, bf16[4,32,256]{2,1,0:T(8,128)(2,1)S(1)} %copy-done.23, bf16[2,32,256]{2,1,0:T(8,128)(2,1)S(1)} %get-tuple-element.33.low_ref, ...), custom_call_target="tpu_custom_call" | custom-call | tf_op jit(solution)/shard_map/window/pallas_call | solution.py:490
  47.6 6.1 %all-to-all-start = ((bf16[32,2,8,512]{3,2,1,0:T(8,128)(2,1)}), bf16[32,2,8,512]{3,2,1,0:T(8,128)(2,1)S(1)}, u32[]{:S(2)}, u32[]{:S(2)}) async-start(bf16[32,2,8,512]{3,2,1,0:T(8,128)(2,1)} %bitcast.56), calls=%async_computation | async-start | bytes 1048576 | tf_op jit(solution)/shard_map/all_to_all | solution.py:476
  58.9 11.9 %window.3 = (f32[8,64,512]{2,1,0:T(8,128)S(1)}, bf16[8,4,2,8,512]{4,3,2,1,0:T(8,128)(2,1)S(1)}) custom-call(s32[4]{0:T(128)S(1)} %copy-done.28, f32[8,64,512]{2,1,0:T(8,128)S(1)} %copy-done.4, bf16[4,32,256]{2,1,0:T(8,128)(2,1)S(1)} %copy-done.22, bf16[2,32,256]{2,1,0:T(8,128)(2,1)S(1)} %copy-done.25, bf16[2,32,256]{2,1,0:T(8,128)(2,1)S(1)} %copy-done.24, ...), custom_call_target="tpu_custom_call" | custom-call | tf_op jit(solution)/shard_map/window/pallas_call | solution.py:490
  72.6 5.9 %all-to-all-start.2 = ((bf16[32,2,8,512]{3,2,1,0:T(8,128)(2,1)}), bf16[32,2,8,512]{3,2,1,0:T(8,128)(2,1)}, u32[]{:S(2)}, u32[]{:S(2)}) async-start(bf16[32,2,8,512]{3,2,1,0:T(8,128)(2,1)} %bitcast.57), calls=%async_computation.2 | async-start | bytes 1048576 | tf_op jit(solution)/shard_map/all_to_all | solution.py:476
  78.8 10.8 %grid.2 = bf16[64,8,512]{2,1,0:T(8,128)(2,1)} custom-call(bf16[64,8,512]{2,1,0:T(8,128)(2,1)S(1)} %bitcast.54, f32[16,8,128]{2,1,0:T(8,128)S(1)} %copy-done.19, bf16[512,1536]{1,0:T(8,128)(2,1)S(1)} %copy-done, bf16[512,512]{1,0:T(8,128)(2,1)S(1)} %bitcast.48), custom_call_target="tpu_custom_call" | custom-call | tf_op jit(solution)/shard_map/grid/pallas_call | solution.py:509
  89.6 4.2 %all-to-all-done.2 = bf16[32,2,8,512]{3,2,1,0:T(8,128)(2,1)} async-done(((bf16[32,2,8,512]{3,2,1,0:T(8,128)(2,1)}), bf16[32,2,8,512]{3,2,1,0:T(8,128)(2,1)}, u32[]{:S(2)}, u32[]{:S(2)}) %all-to-all-start.2) | async-done | bytes 524320 | tf_op jit(solution)/shard_map/all_to_all | solution.py:476
  93.8 3.2 %all-to-all-start.1 = ((bf16[32,2,8,512]{3,2,1,0:T(8,128)(2,1)}), bf16[32,2,8,512]{3,2,1,0:T(8,128)(2,1)S(1)}, u32[]{:S(2)}, u32[]{:S(2)}) async-start(bf16[32,2,8,512]{3,2,1,0:T(8,128)(2,1)} %bitcast.21), calls=%async_computation.1 | async-start | bytes 1048576 | tf_op jit(solution)/shard_map/all_to_all | solution.py:484
  97.0 11.9 %grid.3 = bf16[64,8,512]{2,1,0:T(8,128)(2,1)} custom-call(bf16[64,8,512]{2,1,0:T(8,128)(2,1)} %bitcast.32.cells_ref, f32[16,8,128]{2,1,0:T(8,128)S(1)} %copy-done.19, bf16[512,1536]{1,0:T(8,128)(2,1)S(1)} %copy-done, bf16[512,512]{1,0:T(8,128)(2,1)S(1)} %bitcast.49), custom_call_target="tpu_custom_call" | custom-call | tf_op jit(solution)/shard_map/grid/pallas_call | solution.py:509
  108.9 3.4 %all-to-all-done.1 = bf16[32,2,8,512]{3,2,1,0:T(8,128)(2,1)S(1)} async-done(((bf16[32,2,8,512]{3,2,1,0:T(8,128)(2,1)}), bf16[32,2,8,512]{3,2,1,0:T(8,128)(2,1)S(1)}, u32[]{:S(2)}, u32[]{:S(2)}) %all-to-all-start.1) | async-done | bytes 524320 | tf_op jit(solution)/shard_map/all_to_all | solution.py:484
  112.2 3.3 %all-to-all-start.3 = ((bf16[32,2,8,512]{3,2,1,0:T(8,128)(2,1)}), bf16[32,2,8,512]{3,2,1,0:T(8,128)(2,1)}, u32[]{:S(2)}, u32[]{:S(2)}) async-start(bf16[32,2,8,512]{3,2,1,0:T(8,128)(2,1)} %bitcast.33), calls=%async_computation.3 | async-start | bytes 1048576 | tf_op jit(solution)/shard_map/all_to_all | solution.py:484
  115.6 1.6 %copy-done.2 = bf16[512,2048]{1,0:T(8,128)(2,1)S(1)} copy-done((bf16[512,2048]{1,0:T(8,128)(2,1)S(1)}, bf16[512,2048]{1,0:T(8,128)(2,1)}, u32[]{:S(2)}) %copy-start.2) | copy-done | bytes 2097176
  120.5 8.2 %mlp.2 = f32[8,64,512]{2,1,0:T(8,128)S(1)} custom-call(f32[8,64,512]{2,1,0:T(8,128)S(1)} %copy-done.14, bf16[8,4,2,8,512]{4,3,2,1,0:T(8,128)(2,1)S(1)} %bitcast.55, f32[1,512]{1,0:T(1,128)S(1)} %bitcast.58, bf16[512,512]{1,0:T(8,128)(2,1)S(1)} %copy-done.10, bf16[512,2048]{1,0:T(8,128)(2,1)S(1)} %copy-done.2, bf16[2048,512]{1,0:T(8,128)(2,1)} %second_hbm.3), custom_call_target="tpu_custom_call" | custom-call | tf_op jit(solution)/shard_map/mlp/pallas_call | solution.py:512
  128.7 2.1 %all-to-all-done.3 = bf16[32,2,8,512]{3,2,1,0:T(8,128)(2,1)} async-done(((bf16[32,2,8,512]{3,2,1,0:T(8,128)(2,1)}), bf16[32,2,8,512]{3,2,1,0:T(8,128)(2,1)}, u32[]{:S(2)}, u32[]{:S(2)}) %all-to-all-start.3) | async-done | bytes 524320 | tf_op jit(solution)/shard_map/all_to_all | solution.py:484
  133.0 9.2 %mlp.3 = f32[8,64,512]{2,1,0:T(8,128)S(1)} custom-call(f32[8,64,512]{2,1,0:T(8,128)S(1)} %copy-done.16, bf16[8,4,2,8,512]{4,3,2,1,0:T(8,128)(2,1)} %bitcast.34.heads_ref, f32[1,512]{1,0:T(1,128)S(1)} %bitcast.59, bf16[512,512]{1,0:T(8,128)(2,1)S(1)} %copy-done.11, bf16[512,2048]{1,0:T(8,128)(2,1)S(1)} %copy-done.3, bf16[2048,512]{1,0:T(8,128)(2,1)} %second_hbm.3), custom_call_target="tpu_custom_call" | custom-call | tf_op jit(solution)/shard_map/mlp/pallas_call | solution.py:512
  142.3 1.6 %pad_maximum_fusion = f32[2,8,64,512]{3,2,1,0:T(8,128)} fusion(f32[1,8,64,512]{3,2,1,0:T(8,128)S(1)} %bitcast.53, f32[1,8,64,512]{3,2,1,0:T(8,128)S(1)} %bitcast.52), kind=kLoop, calls=%fused_computation | loop fusion | flops 524288 | bytes 4194304 | tf_op jit(solution)/shard_map/stack | solution.py:515
  (98 shorter events, 29.1 us)
Async XLA Ops:
  1.5 18.5 %collective-permute-start = (bf16[2,2,32,256]{3,2,1,0:T(8,128)(2,1)}, bf16[2,2,32,256]{3,2,1,0:T(8,128)(2,1)}, u32[]{:S(2)}, u32[]{:S(2)}) collective-permute-start(bf16[2,2,32,256]{3,2,1,0:T(8,128)(2,1)} %get-tuple-element.30), channel_id=1, source_target_pairs={{0,4},{4,8},{8,12},{12,16},{16,20},{20,24},{24,28},{1,5},{5,9},{9,... | collective-permute-start | bytes 196616 | tf_op jit(solution)/shard_map/ppermute | solution.py:22
  6.0 16.0 %collective-permute-start.1 = (bf16[2,2,32,256]{3,2,1,0:T(8,128)(2,1)}, bf16[2,2,32,256]{3,2,1,0:T(8,128)(2,1)}, u32[]{:S(2)}, u32[]{:S(2)}) collective-permute-start(bf16[2,2,32,256]{3,2,1,0:T(8,128)(2,1)} %get-tuple-element.29), channel_id=1, source_target_pairs={{4,0},{8,4},{12,8},{16,12},{20,16},{24,20},{28,24},{5,1},{9,5},{13... | collective-permute-start | bytes 196616 | tf_op jit(solution)/shard_map/ppermute | solution.py:25
  12.7 5.5 %copy-start.29 = (f32[2,8,64,512]{3,2,1,0:T(8,128)S(1)}, f32[2,8,64,512]{3,2,1,0:T(8,128)}, u32[]{:S(2)}) copy-start(f32[2,8,64,512]{3,2,1,0:T(8,128)} %param.13) | copy-start | bytes 6291460
  18.1 1.6 %slice-start.1 = ((bf16[512,1536]{1,0:T(8,128)(2,1)}), bf16[512,512]{1,0:T(8,128)(2,1)S(1)}, s32[]{:S(2)}) async-start(bf16[512,1536]{1,0:T(8,128)(2,1)} %qkv_hbm.6), calls=%async_computation.5 | async-start | bytes 1048576 | tf_op jit(solution)/shard_map/slice | solution.py:393
  19.7 11.2 %copy-start.1 = (bf16[512,1536]{1,0:T(8,128)(2,1)S(1)}, bf16[512,1536]{1,0:T(8,128)(2,1)}, u32[]{:S(2)}) copy-start(bf16[512,1536]{1,0:T(8,128)(2,1)} %qkv_hbm.6) | copy-start | bytes 4718596
  19.7 11.2 %copy-start.8 = (bf16[512,512]{1,0:T(8,128)(2,1)S(1)}, bf16[512,512]{1,0:T(8,128)(2,1)}, u32[]{:S(2)}) copy-start(bf16[512,512]{1,0:T(8,128)(2,1)} %out_hbm.6) | copy-start | bytes 1572868
  19.7 11.2 %copy-start.12 = (bf16[8,64,288]{2,1,0:T(8,128)(2,1)S(1)}, bf16[8,64,288]{2,1,0:T(8,128)(2,1)}, u32[]{:S(2)}) copy-start(bf16[8,64,288]{2,1,0:T(8,128)(2,1)} %constant.26.clone.lift_ref) | copy-start | bytes 884740
  20.0 25.8 %copy-start.27 = (s32[4]{0:T(128)}, s32[4]{0:T(128)S(1)}, u32[]{:S(2)}) copy-start(s32[4]{0:T(128)S(1)} %pad_add_fusion.place_ref) | copy-start | bytes 52
  22.9 8.1 %collective-permute-start.3 = (bf16[2,8,2,256]{3,2,1,0:T(2,128)(2,1)S(1)}, bf16[2,8,2,256]{3,2,1,0:T(2,128)(2,1)S(1)}, u32[]{:S(2)}, u32[]{:S(2)}) collective-permute-start(bf16[2,8,2,256]{3,2,1,0:T(2,128)(2,1)S(1)} %get-tuple-element.15), channel_id=1, source_target_pairs={{1,0},{2,1},{3,2},{5,4},{6,5},{7,6},{9,8},{10,9},{11,10},{13,12},{... | collective-permute-start | bytes 49160 | tf_op jit(solution)/shard_map/ppermute | solution.py:25
  24.2 6.8 %collective-permute-start.2 = (bf16[2,8,2,256]{3,2,1,0:T(2,128)(2,1)S(1)}, bf16[2,8,2,256]{3,2,1,0:T(2,128)(2,1)S(1)}, u32[]{:S(2)}, u32[]{:S(2)}) collective-permute-start(bf16[2,8,2,256]{3,2,1,0:T(2,128)(2,1)S(1)} %get-tuple-element.16), channel_id=1, source_target_pairs={{0,1},{1,2},{2,3},{4,5},{5,6},{6,7},{8,9},{9,10},{10,11},{12,13},{... | collective-permute-start | bytes 49160 | tf_op jit(solution)/shard_map/ppermute | solution.py:22
  31.0 1.2 copy-start.5
  33.9 19.9 %copy-start.9 = (bf16[512,512]{1,0:T(8,128)(2,1)S(1)}, bf16[512,512]{1,0:T(8,128)(2,1)}, u32[]{:S(2)}) copy-start(bf16[512,512]{1,0:T(8,128)(2,1)} %out_hbm.6) | copy-start | bytes 1572868
  47.6 24.9 %all-to-all-start = ((bf16[32,2,8,512]{3,2,1,0:T(8,128)(2,1)}), bf16[32,2,8,512]{3,2,1,0:T(8,128)(2,1)S(1)}, u32[]{:S(2)}, u32[]{:S(2)}) async-start(bf16[32,2,8,512]{3,2,1,0:T(8,128)(2,1)} %bitcast.56), calls=%async_computation | async-start | bytes 1048576 | tf_op jit(solution)/shard_map/all_to_all | solution.py:476
  53.8 1.2 copy-start.4
  72.6 5.9 %slice-start = ((bf16[512,1536]{1,0:T(8,128)(2,1)}), bf16[512,512]{1,0:T(8,128)(2,1)S(1)}, s32[]{:S(2)}) async-start(bf16[512,1536]{1,0:T(8,128)(2,1)} %qkv_hbm.7), calls=%async_computation.4 | async-start | bytes 1048576 | tf_op jit(solution)/shard_map/slice | solution.py:394
  72.6 6.2 %copy-start = (bf16[512,1536]{1,0:T(8,128)(2,1)S(1)}, bf16[512,1536]{1,0:T(8,128)(2,1)}, u32[]{:S(2)}) copy-start(bf16[512,1536]{1,0:T(8,128)(2,1)} %qkv_hbm.7) | copy-start | bytes 4718596
  72.6 6.2 %copy-start.19 = (f32[16,8,128]{2,1,0:T(8,128)S(1)}, f32[16,8,128]{2,1,0:T(8,128)}, u32[]{:S(2)}) copy-start(f32[16,8,128]{2,1,0:T(8,128)} %get-tuple-element.27.shifted_ref) | copy-start | bytes 196612
  72.6 21.2 %all-to-all-start.2 = ((bf16[32,2,8,512]{3,2,1,0:T(8,128)(2,1)}), bf16[32,2,8,512]{3,2,1,0:T(8,128)(2,1)}, u32[]{:S(2)}, u32[]{:S(2)}) async-start(bf16[32,2,8,512]{3,2,1,0:T(8,128)(2,1)} %bitcast.57), calls=%async_computation.2 | async-start | bytes 1048576 | tf_op jit(solution)/shard_map/all_to_all | solution.py:476
  93.8 18.4 %all-to-all-start.1 = ((bf16[32,2,8,512]{3,2,1,0:T(8,128)(2,1)}), bf16[32,2,8,512]{3,2,1,0:T(8,128)(2,1)S(1)}, u32[]{:S(2)}, u32[]{:S(2)}) async-start(bf16[32,2,8,512]{3,2,1,0:T(8,128)(2,1)} %bitcast.21), calls=%async_computation.1 | async-start | bytes 1048576 | tf_op jit(solution)/shard_map/all_to_all | solution.py:484
  97.0 18.6 %copy-start.26 = (f32[512]{0:T(512)S(1)}, f32[512]{0:T(512)}, u32[]{:S(2)}) copy-start(f32[512]{0:T(512)} %param.22) | copy-start | bytes 6148
  112.2 3.3 %copy-start.6 = (bf16[32,2,8,512]{3,2,1,0:T(8,128)(2,1)}, bf16[32,2,8,512]{3,2,1,0:T(8,128)(2,1)S(1)}, u32[]{:S(2)}) copy-start(bf16[32,2,8,512]{3,2,1,0:T(8,128)(2,1)S(1)} %all-to-all-done.1) | copy-start | bytes 1572868
  112.2 18.5 %all-to-all-start.3 = ((bf16[32,2,8,512]{3,2,1,0:T(8,128)(2,1)}), bf16[32,2,8,512]{3,2,1,0:T(8,128)(2,1)}, u32[]{:S(2)}, u32[]{:S(2)}) async-start(bf16[32,2,8,512]{3,2,1,0:T(8,128)(2,1)} %bitcast.33), calls=%async_computation.3 | async-start | bytes 1048576 | tf_op jit(solution)/shard_map/all_to_all | solution.py:484
  115.6 1.6 %copy-start.2 = (bf16[512,2048]{1,0:T(8,128)(2,1)S(1)}, bf16[512,2048]{1,0:T(8,128)(2,1)}, u32[]{:S(2)}) copy-start(bf16[512,2048]{1,0:T(8,128)(2,1)} %first_hbm.3) | copy-start | bytes 6291460
  120.5 10.3 %copy-start.3 = (bf16[512,2048]{1,0:T(8,128)(2,1)S(1)}, bf16[512,2048]{1,0:T(8,128)(2,1)}, u32[]{:S(2)}) copy-start(bf16[512,2048]{1,0:T(8,128)(2,1)} %first_hbm.3) | copy-start | bytes 6291460
  (16 other events, 14.7 us)
where the time goes:
time: 146 us; the launch traced here: 144 us
  Pallas kernels  63.9 us (44%)
  local copies, waits for them, and re-layouts  38 us (26%)
  starting transfers between devices  30.2 us (21%)
  waiting for transfers between devices  9.71 us (7%)
  other arithmetic  1.64 us (1%)
    pallas_call x2, Pallas kernels, on_device(): window_call(place, latent[sample], context[sample], low[sample], high[sam...  23.8 us
    pallas_call x2, Pallas kernels, on_device(): heads = grid_call(cells[sample], grid_shifted, grid_qkv, grid_vt)  22.7 us
    unnamed x65, local copies, waits for them, and re-layouts  22 us
    pallas_call x2, Pallas kernels, on_device(): mlp_call(residuals[sample], returned[sample], gain, grid_out, mlp_in, mlp...  17.4 us
    all_to_all x2, starting transfers between devices, send(): lax.all_to_all(pieces, JOINT, split_axis=0, concat_axis=0, tiled=True)  12 us
    ppermute x2, starting transfers between devices, neighbours(): lax.ppermute(lax.slice_in_dim(block, block.shape[dim] - width, None, axis...  8.47 us
    all_to_all x2, starting transfers between devices, send_back(): lax.all_to_all(pieces, JOINT, split_axis=0, concat_axis=0, tiled=True)  6.45 us
    all_to_all x2, waiting for transfers between devices, send_back(): lax.all_to_all(pieces, JOINT, split_axis=0, concat_axis=0, tiled=True)  5.47 us
  transfers between devices with their start and end apart: 8, of which 3 were waited for; matrix products, arithmetic and copies ran while one was open for 12% of the time, Pallas kernels for 30%

commit v1 on v0

v1 whole, which is shorter than its diff:
```python
import functools
import math

import jax
import jax.numpy as jnp
import numpy as np
from jax import lax
from jax.experimental import pallas as pl
from jax.experimental.pallas import tpu as pltpu
from jax.sharding import PartitionSpec as P

HEAD = 32
WIN = 8
NORM_EPS = 1e-05
LANES = 128
LOG2E = math.log2(math.e)
JOINT = ("wide", "narrow")


def neighbours(block, axis, dim, width):
    count = lax.axis_size(axis)
    forward = [(i, i + 1) for i in range(count - 1)]
    backward = [(target, source) for source, target in forward]
    low = lax.ppermute(
        lax.slice_in_dim(block, block.shape[dim] - width, None, axis=dim), axis, forward
    )
    high = lax.ppermute(lax.slice_in_dim(block, 0, width, axis=dim), axis, backward)
    return low, high


def bias_kernel(flat_ref, pick_ref, window_ref, grid_ref, spread_s):
    both, places = flat_ref.shape
    side = WIN
    flat = flat_ref[...] * LOG2E
    top = flat.astype(jnp.bfloat16)
    rest = flat - top.astype(jnp.float32)
    middle = rest.astype(jnp.bfloat16)
    last = (rest - middle.astype(jnp.float32)).astype(jnp.bfloat16)
    stacked = jnp.concatenate([top, middle, last], axis=0)
    for key_col in range(side):
        picked = jnp.dot(stacked, pick_ref[key_col], preferred_element_type=jnp.float32)
        spread_s[pl.ds(key_col, both, stride=side), :] = (
            picked[:both] + picked[both : 2 * both]
        ) + picked[2 * both :]
    low_half = lax.broadcasted_iota(jnp.int32, (side, LANES), 1) < side * side
    heads = both // 2
    for table, table_ref in enumerate((window_ref, grid_ref)):
        for pair in range(heads // 2):
            base = (table * heads + 2 * pair) * side
            even = spread_s[base : base + side]
            odd = spread_s[base + side : base + 2 * side]
            for key_row in range(side):
                start = side * (side - 1 - key_row)
                even_part = pltpu.roll(even, (LANES - start) % LANES, 1)
                odd_part = pltpu.roll(odd, (LANES - start + side * side) % LANES, 1)
                table_ref[
                    key_row * side : (key_row + 1) * side, pair * LANES : (pair + 1) * LANES
                ] = jnp.where(low_half, even_part, odd_part)


def bias_pick(places):
    side = WIN
    span = 2 * side - 1
    pick = np.zeros((side, places, LANES), np.float32)
    for c in range(side):
        for a in range(span):
            for j in range(side):
                pick[c, a * span + j + side - 1 - c, a * side + j] = 1.0
    return jnp.asarray(pick, jnp.bfloat16)


def layer_norm(values):
    center = values - jnp.mean(values, axis=-1, keepdims=True)
    spread = jnp.mean(center * center, axis=-1, keepdims=True)
    return center * lax.rsqrt(spread + NORM_EPS)


def project(normed_s, qk_w, vt_w, qk_s, vt_s, waits):
    channels = normed_s.shape[1]
    waits[0].wait()
    queries = jnp.dot(
        normed_s[...], qk_w[:, :channels], preferred_element_type=jnp.float32
    )
    qk_s[:, :channels] = (queries * (LOG2E * HEAD ** (-0.5))).astype(jnp.bfloat16)
    qk_s[:, channels:] = jnp.dot(
        normed_s[...], qk_w[:, channels:], preferred_element_type=jnp.float32
    ).astype(jnp.bfloat16)
    waits[1].wait()
    values = lax.dot_general(
        vt_w[...], normed_s[...], (((1,), (1,)), ((), ())), preferred_element_type=jnp.float32
    ).astype(jnp.bfloat16)
    pairs, tall = vt_s.shape[:2]
    for pair in range(pairs):
        vt_s[pair, : 2 * HEAD] = values[pair * 2 * HEAD : (pair + 1) * 2 * HEAD]
        vt_s[pair, 2 * HEAD :] = jnp.ones((tall - 2 * HEAD, values.shape[1]), jnp.bfloat16)


def attend(groups, qk_s, vt_s, bias_s, score_s, top_s, lifted_s, store):
    members = WIN * WIN
    channels = qk_s.shape[1] // 2
    blocks = channels // LANES
    per = LANES // HEAD
    wide = per * members
    lane_head = lax.broadcasted_iota(jnp.int32, (members, LANES), 1) // HEAD
    own = [lane_head == h for h in range(per)]
    low_half = lax.broadcasted_iota(jnp.int32, (HEAD, LANES), 1) < members

    def scores(group, block):
        rows = slice(group * members, (group + 1) * members)
        part = slice(block * wide, (block + 1) * wide)
        queries = qk_s[rows, block * LANES : (block + 1) * LANES]
        keys = qk_s[rows, channels + block * LANES : channels + (block + 1) * LANES]
        zero = jnp.zeros_like(queries)
        spread = jnp.concatenate([jnp.where(mask, queries, zero) for mask in own], axis=0)
        score = lax.dot_general(
            keys, spread, (((1,), (1,)), ((), ())), preferred_element_type=jnp.float32
        )
        score = score + bias_s[:, part]
        score_s[group % 2, :, part] = score
        top_s[group % 2, :, part] = jnp.max(score, axis=0, keepdims=True)

    def lift(group, block):
        part = slice(block * wide, (block + 1) * wide)
        lifted = jnp.exp2(score_s[group % 2, :, part] - top_s[group % 2, :, part])
        lifted_s[group % 2, :, part] = lifted.astype(jnp.bfloat16)

    def blend(group, block):
        pieces = []
        for pair in range(block * per // 2, (block + 1) * per // 2):
            values = vt_s[pair, :, group * members : (group + 1) * members]
            mixed = jnp.dot(
                values,
                lifted_s[group % 2, :, pair * LANES : (pair + 1) * LANES],
                preferred_element_type=jnp.float32,
            )
            chosen = jnp.where(low_half, mixed[:HEAD], mixed[HEAD : 2 * HEAD])
            pieces.append(chosen * (1.0 / mixed[2 * HEAD : 2 * HEAD + 1]))
        return pieces

    for step in range(groups + 2):
        pieces = []
        for block in range(blocks):
            if step < groups:
                scores(step, block)
            if 0 <= step - 1 < groups:
                lift(step - 1, block)
            if step >= 2:
                pieces.extend(blend(step - 2, block))
        if pieces:
            turned = jnp.concatenate(pieces, axis=0).T
            store(step - 2, jnp.concatenate([turned[:members], turned[members:]], axis=1))


def out_copies(weight_ref, buffer_ref, sem):
    pairs = weight_ref.shape[0] // (2 * HEAD)
    return [
        pltpu.make_async_copy(
            weight_ref.at[pl.ds((2 * pair + parity) * HEAD, HEAD)],
            buffer_ref.at[pl.ds((parity * pairs + pair) * HEAD, HEAD)],
            sem,
        )
        for parity in range(2)
        for pair in range(pairs)
    ]


def window_kernel(
    place_ref,
    latent_hbm,
    context_hbm,
    low_hbm,
    high_hbm,
    left_hbm,
    right_hbm,
    lift_hbm,
    bias_hbm,
    conv_hbm,
    qkv_hbm,
    vt_hbm,
    out_hbm,
    residual_hbm,
    normed_hbm,
    latent_ref,
    context_ref,
    low_ref,
    high_ref,
    left_ref,
    right_ref,
    lift_ref,
    bias_s,
    conv_w,
    qk_w,
    vt_w,
    out_w,
    wide_s,
    taps_s,
    features_s,
    residual_ref,
    normed_s,
    qk_s,
    vt_s,
    score_s,
    top_s,
    lifted_s,
    heads_s,
    sent_s,
    sems,
    out_sems,
    *,
    stride,
    sample,
):
    rows, cols, channels = latent_ref.shape
    half_rows, half_cols, coarse = context_ref.shape
    members = WIN * WIN
    windows = cols // WIN
    halo = [
        pltpu.make_async_copy(source.at[sample], target, sems.at[0])
        for source, target in (
            (context_hbm, context_ref),
            (low_hbm, low_ref),
            (high_hbm, high_ref),
            (left_hbm, left_ref),
            (right_hbm, right_ref),
        )
    ]
    conv_copy = pltpu.make_async_copy(conv_hbm, conv_w, sems.at[1])
    cells_copies = [
        pltpu.make_async_copy(lift_hbm, lift_ref, sems.at[2]),
        pltpu.make_async_copy(latent_hbm.at[sample], latent_ref, sems.at[2]),
    ]
    qk_copy = pltpu.make_async_copy(qkv_hbm.at[:, pl.ds(0, 2 * channels)], qk_w, sems.at[3])
    vt_copy = pltpu.make_async_copy(vt_hbm, vt_w, sems.at[4])
    bias_copy = pltpu.make_async_copy(bias_hbm, bias_s, sems.at[5])
    placed = out_copies(out_hbm, out_w, sems.at[6])
    for copy in halo + [conv_copy] + cells_copies + [qk_copy, vt_copy, bias_copy] + placed:
        copy.start()
    span = half_rows + 2
    for copy in halo:
        copy.wait()
    for row in range(half_rows + 4):
        base = row * stride
        if row < 2:
            middle = low_ref[row]
        elif row < half_rows + 2:
            middle = context_ref[row - 2]
        else:
            middle = high_ref[row - half_rows - 2]
        wide_s[base + 6 : base + 8] = left_ref[row].astype(jnp.float32)
        wide_s[base + 8 : base + 8 + half_cols] = middle.astype(jnp.float32)
        wide_s[base + 8 + half_cols : base + 10 + half_cols] = right_ref[row].astype(jnp.float32)
    tall = (half_rows + 4) * stride
    for shift in range(3):
        taps_s[:, shift * coarse : (shift + 1) * coarse] = wide_s[
            shift + 6 : shift + 6 + tall
        ].astype(jnp.bfloat16)
    conv_copy.wait()
    patches = jnp.concatenate(
        [taps_s[shift * stride : (shift + span) * stride] for shift in range(3)], axis=1
    )
    total = jnp.dot(patches, conv_w[...], preferred_element_type=jnp.float32)
    column = lax.broadcasted_iota(jnp.int32, (stride, channels), 0)
    col_place = column + place_ref[1]
    col_inside = (col_place >= 0) & (col_place < place_ref[3]) & (column < half_cols + 2)
    for row in range(span):
        row_place = place_ref[0] + row
        inside = col_inside & ((row_place >= 0) & (row_place < place_ref[2]))
        part = slice(row * stride, (row + 1) * stride)
        features_s[part] = jnp.where(inside, total[part], 0.0).astype(jnp.bfloat16)

    for copy in cells_copies:
        copy.wait()
    residual_ref[...] = jnp.dot(
        lift_ref[...], features_s[...], preferred_element_type=jnp.float32
    )
    for window in range(windows):
        part = slice(window * members, (window + 1) * members)
        cells = latent_ref[:, window * WIN : (window + 1) * WIN, :].reshape(members, channels)
        residual = cells + residual_ref[part]
        residual_ref[part] = residual
        normed_s[part] = layer_norm(residual).astype(jnp.bfloat16)

    project(normed_s, qk_w, vt_w, qk_s, vt_s, (qk_copy, vt_copy))
    bias_copy.wait()

    def store_heads(window, heads):
        heads_s[window * members : (window + 1) * members] = heads.astype(jnp.bfloat16)

    attend(windows, qk_s, vt_s, bias_s, score_s, top_s, lifted_s, store_heads)
    for copy in placed:
        copy.wait()
    residual_ref[...] += jnp.dot(heads_s[...], out_w[...], preferred_element_type=jnp.float32)
    narrow = normed_hbm.shape[1]
    for window in range(windows):
        part = slice(window * members, (window + 1) * members)
        normed = layer_norm(residual_ref[part]).astype(jnp.bfloat16)
        sent_s[:, window % narrow, window // narrow] = normed.reshape(rows, WIN, channels)
    stores = [
        pltpu.make_async_copy(sent_s, normed_hbm, out_sems.at[0]),
        pltpu.make_async_copy(residual_ref, residual_hbm, out_sems.at[1]),
    ]
    for store in stores:
        store.start()
    for store in stores:
        store.wait()


def grid_kernel(
    cells_hbm,
    bias_hbm,
    qkv_hbm,
    vt_hbm,
    heads_hbm,
    cells_ref,
    qk_w,
    vt_w,
    spread_s,
    normed_s,
    qk_s,
    vt_s,
    score_s,
    top_s,
    lifted_s,
    bias_s,
    sems,
):
    tokens, channels = cells_ref.shape
    groups = WIN
    members = tokens // groups
    copies = [
        pltpu.make_async_copy(cells_hbm, cells_ref, sems.at[0]),
        pltpu.make_async_copy(qkv_hbm.at[:, pl.ds(0, 2 * channels)], qk_w, sems.at[1]),
        pltpu.make_async_copy(vt_hbm, vt_w, sems.at[2]),
        pltpu.make_async_copy(bias_hbm, bias_s, sems.at[3]),
    ]
    for copy in copies:
        copy.start()
    copies[0].wait()
    lanes = [slice(start, start + LANES) for start in range(0, channels, LANES)]
    for chunk, lane in enumerate(lanes):
        spread_s[chunk] = cells_ref[:, lane].astype(jnp.float32)
    for group in range(groups):
        for chunk, lane in enumerate(lanes):
            normed_s[group * members : (group + 1) * members, lane] = spread_s[
                chunk, pl.ds(group, members, stride=groups), :
            ].astype(jnp.bfloat16)
    project(normed_s, qk_w, vt_w, qk_s, vt_s, copies[1:3])
    copies[3].wait()

    def store_heads(group, heads):
        for chunk, lane in enumerate(lanes):
            spread_s[chunk, pl.ds(group, members, stride=groups), :] = heads[:, lane]

    attend(groups, qk_s, vt_s, bias_s, score_s, top_s, lifted_s, store_heads)
    for chunk, lane in enumerate(lanes):
        cells_ref[:, lane] = spread_s[chunk].astype(jnp.bfloat16)
    store = pltpu.make_async_copy(cells_ref, heads_hbm, sems.at[0])
    store.start()
    store.wait()


def mlp_kernel(
    *refs,
    sample,
):
    (
        residual_hbm,
        heads_hbm,
        gain_ref,
        out_hbm,
        first_hbm,
        second_hbm,
    ) = refs[:6]
    (
        result_hbm,
        residual_ref,
        heads_ref,
        out_w,
        first_w,
        second_w,
        residual_s,
        normed_s,
        active_s,
        sems,
    ) = refs[-10:]
    tokens, channels = residual_ref.shape
    members = WIN * WIN
    windows = tokens // members
    rows, narrow = heads_ref.shape[:2]
    hidden = first_w.shape[1]
    placed = out_copies(out_hbm, out_w, sems.at[0])
    cells = [
        pltpu.make_async_copy(heads_hbm, heads_ref, sems.at[3]),
        pltpu.make_async_copy(residual_hbm, residual_ref, sems.at[4]),
    ]
    copies = [
        pltpu.make_async_copy(first_hbm, first_w, sems.at[1]),
        pltpu.make_async_copy(second_hbm, second_w, sems.at[2]),
    ]
    for copy in placed + cells + copies:
        copy.start()
    for copy in placed + cells:
        copy.wait()
    for window in range(windows):
        part = slice(window * members, (window + 1) * members)
        heads = heads_ref[:, window % narrow, window // narrow]
        normed_s[part] = heads.reshape(members, channels)
    residual_s[...] = residual_ref[...] + jnp.dot(
        normed_s[...], out_w[...], preferred_element_type=jnp.float32
    )
    for window in range(windows):
        part = slice(window * members, (window + 1) * members)
        normed_s[part] = (layer_norm(residual_s[part]) * gain_ref[...]).astype(jnp.bfloat16)
    copies[0].wait()
    for start in range(0, hidden, channels):
        part = slice(start, start + channels)
        inner = jnp.dot(normed_s[...], first_w[:, part], preferred_element_type=jnp.float32)
        root = 0.7978845608028654
        angle = inner * (root + (root * 0.044715) * (inner * inner))
        halved = 0.5 * inner
        active_s[:, part] = (halved + halved * jnp.tanh(angle)).astype(jnp.bfloat16)
    copies[1].wait()
    residual_s[...] += jnp.dot(active_s[...], second_w[...], preferred_element_type=jnp.float32)
    stores = []
    for window in range(windows):
        store = pltpu.make_async_copy(
            residual_s.at[pl.ds(window * members, members)].reshape(rows, WIN, channels),
            result_hbm.at[sample, :, pl.ds(window * WIN, WIN), :],
            sems.at[0],
        )
        store.start()
        stores.append(store)
    for store in stores:
        store.wait()


VMEM = pl.BlockSpec(memory_space=pltpu.MemorySpace.VMEM)
HBM = pl.BlockSpec(memory_space=pltpu.MemorySpace.HBM)
SMEM = pl.BlockSpec(memory_space=pltpu.MemorySpace.SMEM)
PARAMS = dict(vmem_limit_bytes=48 * 1024 * 1024)


def pinned(call, *arrays):
    return call(
        *(
            pltpu.with_memory_space_constraint(a, pltpu.HBM) if a.size > 1024 else a
            for a in arrays
        )
    )


def lift_matrix(rows, cols, stride):
    def along(count):
        fine = np.arange(count)
        place = np.zeros((count, count // 2 + 2), np.float32)
        middle = fine // 2 + 1
        place[fine, middle] = 0.75
        place[fine, middle + np.where(fine % 2 == 0, -1, 1)] = 0.25
        return place

    by_row = along(rows)
    by_col = along(cols)
    by_col = np.pad(by_col, ((0, 0), (0, stride - by_col.shape[1])))
    both = by_row[:, None, :, None] * by_col[None, :, None, :]
    both = both.reshape(rows, cols // WIN, WIN, -1).transpose(1, 0, 2, 3)
    return jnp.asarray(both.reshape(rows * cols, -1), jnp.bfloat16)


def on_device(
    latent,
    context,
    conv_weight,
    window_qkv,
    window_out,
    window_bias,
    grid_qkv,
    grid_out,
    grid_bias,
    mlp_gain,
    mlp_in,
    mlp_out,
):
    samples, rows, cols, channels = latent.shape
    wide_count = lax.axis_size("wide")
    narrow = lax.axis_size("narrow")
    half_rows, half_cols, coarse = context.shape[1:]
    hidden = mlp_in.shape[1]
    members = WIN * WIN
    windows = cols // WIN
    planes = WIN // narrow
    split = wide_count // WIN
    assert rows == WIN and planes * narrow == WIN and split * WIN == wide_count
    assert windows == planes * narrow and WIN % split == 0
    stride = -(-(half_cols + 10) // 16) * 16

    low, high = neighbours(context, "wide", 1, 2)
    parts = (low, context, high)
    forward = [(i, i + 1) for i in range(narrow - 1)]
    backward = [(target, source) for source, target in forward]
    left = lax.ppermute(
        jnp.concatenate([part[:, :, half_cols - 2 :] for part in parts], axis=1), "narrow", forward
    )
    right = lax.ppermute(
        jnp.concatenate([part[:, :, :2] for part in parts], axis=1), "narrow", backward
    )
    heads_count = window_bias.shape[0]
    places = window_bias.shape[1] * window_bias.shape[2]
    flat_bias = jnp.concatenate([window_bias, grid_bias], axis=0).reshape(-1, places)
    table = jax.ShapeDtypeStruct((WIN * WIN, heads_count * WIN * WIN), jnp.float32)
    window_table, grid_table = pl.pallas_call(
        bias_kernel,
        out_shape=(table, table),
        in_specs=[VMEM, VMEM],
        out_specs=(VMEM, VMEM),
        scratch_shapes=[pltpu.VMEM((2 * heads_count * WIN, LANES), jnp.float32)],
        compiler_params=pltpu.CompilerParams(**PARAMS),
        name="bias",
    )(flat_bias, bias_pick(places))
    window_vt = window_qkv[:, 2 * channels :].T
    grid_vt = grid_qkv[:, 2 * channels :].T
    lift = lift_matrix(rows, cols, stride)
    conv_flat = conv_weight.reshape(9 * coarse, channels)
    place = jnp.stack(
        [
            lax.axis_index("wide") * half_rows - 1,
            lax.axis_index("narrow") * half_cols - 1,
            jnp.int32(wide_count * half_rows),
            jnp.int32(narrow * half_cols),
        ]
    ).astype(jnp.int32)

    bf16, f32 = jnp.bfloat16, jnp.float32
    tokens = rows * cols
    span = half_rows + 2
    def window_call(sample):
        return pl.pallas_call(
            functools.partial(window_kernel, stride=stride, sample=sample),
            out_shape=(
                pltpu.HBM((tokens, channels), f32),
                pltpu.HBM((rows, narrow, planes, WIN, channels), bf16),
            ),
            in_specs=[SMEM] + [HBM] * 12,
            out_specs=(HBM, HBM),
            scratch_shapes=[
                pltpu.VMEM((rows, cols, channels), f32),
                pltpu.VMEM((half_rows, half_cols, coarse), bf16),
                pltpu.VMEM((2, half_cols, coarse), bf16),
                pltpu.VMEM((2, half_cols, coarse), bf16),
                pltpu.VMEM((half_rows + 4, 2, coarse), bf16),
                pltpu.VMEM((half_rows + 4, 2, coarse), bf16),
                pltpu.VMEM((tokens, span * stride), bf16),
                pltpu.VMEM((members, heads_count * members), f32),
                pltpu.VMEM((9 * coarse, channels), bf16),
                pltpu.VMEM((channels, 2 * channels), bf16),
                pltpu.VMEM((channels, channels), bf16),
                pltpu.VMEM((channels, channels), bf16),
                pltpu.VMEM(((half_rows + 4) * stride + 16, coarse), f32),
                pltpu.VMEM(((half_rows + 4) * stride, 3 * coarse), bf16),
                pltpu.VMEM((span * stride, channels), bf16),
                pltpu.VMEM((tokens, channels), f32),
                pltpu.VMEM((tokens, channels), bf16),
                pltpu.VMEM((tokens, 2 * channels), bf16),
                pltpu.VMEM((heads_count // 2, 2 * HEAD + 16, tokens), bf16),
                pltpu.VMEM((2, members, heads_count * members), f32),
                pltpu.VMEM((2, 1, heads_count * members), f32),
                pltpu.VMEM((2, members, heads_count * members), bf16),
                pltpu.VMEM((tokens, channels), bf16),
                pltpu.VMEM((rows, narrow, planes, WIN, channels), bf16),
                pltpu.SemaphoreType.DMA((7,)),
                pltpu.SemaphoreType.DMA((2,)),
            ],
            compiler_params=pltpu.CompilerParams(**PARAMS),
            name="window",
        )

    grid_call = pl.pallas_call(
        grid_kernel,
        out_shape=pltpu.HBM((tokens, channels), bf16),
        in_specs=[HBM] * 4,
        out_specs=HBM,
        scratch_shapes=[
            pltpu.VMEM((tokens, channels), bf16),
            pltpu.VMEM((channels, 2 * channels), bf16),
            pltpu.VMEM((channels, channels), bf16),
            pltpu.VMEM((channels // LANES, tokens, LANES), f32),
            pltpu.VMEM((tokens, channels), bf16),
            pltpu.VMEM((tokens, 2 * channels), bf16),
            pltpu.VMEM((heads_count // 2, 2 * HEAD + 16, tokens), bf16),
            pltpu.VMEM((2, members, heads_count * members), f32),
            pltpu.VMEM((2, 1, heads_count * members), f32),
            pltpu.VMEM((2, members, heads_count * members), bf16),
            pltpu.VMEM((members, heads_count * members), f32),
            pltpu.SemaphoreType.DMA((4,)),
        ],
        compiler_params=pltpu.CompilerParams(**PARAMS),
        name="grid",
    )

    def mlp_call(sample):
        first = sample == 0
        return pl.pallas_call(
            functools.partial(mlp_kernel, sample=sample),
            out_shape=pltpu.HBM((samples, rows, cols, channels), f32),
            in_specs=[HBM, HBM, VMEM] + [HBM] * (3 if first else 4),
            out_specs=HBM,
            input_output_aliases={} if first else {6: 0},
            scratch_shapes=[
                pltpu.VMEM((tokens, channels), f32),
                pltpu.VMEM((rows, narrow, planes, WIN, channels), bf16),
                pltpu.VMEM((channels, channels), bf16),
                pltpu.VMEM((channels, hidden), bf16),
                pltpu.VMEM((hidden, channels), bf16),
                pltpu.VMEM((tokens, channels), f32),
                pltpu.VMEM((tokens, channels), bf16),
                pltpu.VMEM((tokens, hidden), bf16),
                pltpu.SemaphoreType.DMA((5,)),
            ],
            compiler_params=pltpu.CompilerParams(**PARAMS),
            name="mlp",
        )

    gain = mlp_gain.reshape(1, channels)

    def send(normed):
        pieces = normed.reshape(rows, narrow, planes, split, WIN // split, channels)
        pieces = pieces.transpose(0, 3, 1, 2, 4, 5)
        pieces = pieces.reshape(wide_count * narrow, planes, WIN // split, channels)
        received = lax.all_to_all(pieces, JOINT, split_axis=0, concat_axis=0, tiled=True)
        received = received.reshape(WIN, split, narrow, planes, WIN // split, channels)
        return received.transpose(0, 2, 3, 1, 4, 5).reshape(tokens, channels)

    def send_back(heads):
        pieces = heads.reshape(WIN, narrow, planes, split, WIN // split, channels)
        pieces = pieces.transpose(0, 3, 1, 2, 4, 5)
        pieces = pieces.reshape(wide_count * narrow, planes, WIN // split, channels)
        received = lax.all_to_all(pieces, JOINT, split_axis=0, concat_axis=0, tiled=True)
        received = received.reshape(rows, split, narrow, planes, WIN // split, channels)
        return received.transpose(0, 2, 3, 1, 4, 5).reshape(rows, narrow, planes, WIN, channels)

    residuals, cells = [], []
    for sample in range(samples):
        residual, normed = pinned(
            window_call(sample),
            place,
            latent,
            context,
            low,
            high,
            left,
            right,
            lift,
            window_table,
            conv_flat,
            window_qkv,
            window_vt,
            window_out,
        )
        residuals.append(residual)
        cells.append(send(normed))
    returned = []
    for sample in range(samples):
        heads = pinned(grid_call, cells[sample], grid_table, grid_qkv, grid_vt)
        returned.append(send_back(heads))
    result = ()
    for sample in range(samples):
        result = (
            pinned(
                mlp_call(sample), residuals[sample], returned[sample], gain, grid_out, mlp_in, mlp_out, *result
            ),
        )
    return result[0]


def solution(mesh):
    return jax.shard_map(
        on_device,
        mesh=mesh,
        in_specs=(
            P(None, "wide", "narrow", None),
            P(None, "wide", "narrow", None),
        )
        + (P(),) * 10,
        out_specs=P(None, "wide", "narrow", None),
        check_vma=False,
    )
```

time: 146 us -> 113 us (0.77)
  local copies, waits for them, and re-layouts: 38 us -> 6.21 us
  waiting for transfers between devices: 9.71 us -> 35.4 us
  Pallas kernels: 63.9 us -> 40.9 us
  starting transfers between devices: 30.2 us -> 28.1 us
    pallas_call x6 -> x7, Pallas kernels: 63.9 us -> 40.9 us  [the longest x6 40.3 us: pinned(): call(*(pltpu.with_memory_space_constraint(a, pltpu.HBM) if a.size > 1024...]
    unnamed x65 -> x26, local copies, waits for them, and re-layouts: 22 us -> 4.13 us
    all_to_all x2, waiting for transfers between devices: 5.47 us -> 18.8 us  [send_back(): lax.all_to_all(pieces, JOINT, split_axis=0, concat_axis=0, tiled=True)]
    all_to_all x2, waiting for transfers between devices: 4.23 us -> 15.8 us  [send(): lax.all_to_all(pieces, JOINT, split_axis=0, concat_axis=0, tiled=True)]
    squeeze x6 -> x0, local copies, waits for them, and re-layouts: 5.9 us -> none  [the longest x1 1.59 us: on_device(): latent[sample]]
    slice x10 -> x3, local copies, waits for them, and re-layouts: 6.06 us -> 0.82 us  [on_device(): part[:, :, :2]]
    ppermute x0 -> x2, starting transfers between devices: none -> 4.49 us  [the longest x1 3.2 us: on_device(): lax.ppermute(jnp.concatenate([part[:, :, half_cols - 2:] for part in part...]
    ppermute x2 -> x1, starting transfers between devices: 8.47 us -> 4.49 us  [neighbours(): lax.ppermute(lax.slice_in_dim(block, block.shape[dim] - width, None, axis...]
  transfers between devices with their start and end apart: 8 -> 8, of which waited for: 3 -> 5; matrix products, arithmetic and copies ran while one was open for 12% -> 4% of each run, Pallas kernels for 30% -> 23%
where the time goes in v1:
time: 113 us; the launch traced here: 112 us
  Pallas kernels  40.9 us (36%)
  waiting for transfers between devices  35.4 us (31%)
  starting transfers between devices  28.1 us (25%)
  local copies, waits for them, and re-layouts  6.21 us (5%)
    pallas_call x6, Pallas kernels, pinned(): call(*(pltpu.with_memory_space_constraint(a, pltpu.HBM) if a.size > 1024...  40.3 us
    all_to_all x2, waiting for transfers between devices, send_back(): lax.all_to_all(pieces, JOINT, split_axis=0, concat_axis=0, tiled=True)  18.8 us
    all_to_all x2, waiting for transfers between devices, send(): lax.all_to_all(pieces, JOINT, split_axis=0, concat_axis=0, tiled=True)  15.8 us
    all_to_all x2, starting transfers between devices, send(): lax.all_to_all(pieces, JOINT, split_axis=0, concat_axis=0, tiled=True)  10.9 us
    all_to_all x2, starting transfers between devices, send_back(): lax.all_to_all(pieces, JOINT, split_axis=0, concat_axis=0, tiled=True)  6.3 us
    ppermute x1, starting transfers between devices, neighbours(): lax.ppermute(lax.slice_in_dim(block, block.shape[dim] - width, None, axis...  4.49 us
    unnamed x26, local copies, waits for them, and re-layouts  4.13 us
    ppermute x1, starting transfers between devices, on_device(): lax.ppermute(jnp.concatenate([part[:, :, half_cols - 2:] for part in part...  3.2 us
  transfers between devices with their start and end apart: 8, of which 5 were waited for; matrix products, arithmetic and copies ran while one was open for 4% of the time, Pallas kernels for 23%

profile of v1, /device:TPU:1, one launch (start us, length us, event | category | flops | bytes accessed | tf_op | source)
XLA Modules:
  0.0 112.3 jit_solution(12262664984196642055)
XLA Ops:
  0.0 1.0 fusion.1
  1.0 1.9 %collective-permute-start.1 = (bf16[2,2,32,256]{3,2,1,0:T(8,128)(2,1)S(1)}, bf16[2,2,32,256]{3,2,1,0:T(8,128)(2,1)S(1)}, u32[]{:S(2)}, u32[]{:S(2)}) collective-permute-start(bf16[2,2,32,256]{3,2,1,0:T(8,128)(2,1)S(1)} %get-tuple-element.19), channel_id=1, source_target_pairs={{4,0},{8,4},{12,8},{16,12},{20,16},{24,20},{28,24},{5,1},{9,5},{13... | collective-permute-start | bytes 196616 | tf_op jit(solution)/shard_map/ppermute | solution.py:27
  2.9 4.5 %collective-permute-start = (bf16[2,2,32,256]{3,2,1,0:T(8,128)(2,1)S(1)}, bf16[2,2,32,256]{3,2,1,0:T(8,128)(2,1)S(1)}, u32[]{:S(2)}, u32[]{:S(2)}) collective-permute-start(bf16[2,2,32,256]{3,2,1,0:T(8,128)(2,1)S(1)} %get-tuple-element.20), channel_id=1, source_target_pairs={{0,4},{4,8},{8,12},{12,16},{16,20},{20,24},{24,28},{1,5},{5,9},{9,... | collective-permute-start | bytes 196616 | tf_op jit(solution)/shard_map/ppermute | solution.py:24
  8.2 1.0 pad_maximum_fusion
  9.3 3.2 %collective-permute-start.2 = (bf16[2,8,2,256]{3,2,1,0:T(2,128)(2,1)S(1)}, bf16[2,8,2,256]{3,2,1,0:T(2,128)(2,1)S(1)}, u32[]{:S(2)}, u32[]{:S(2)}) collective-permute-start(bf16[2,8,2,256]{3,2,1,0:T(2,128)(2,1)S(1)} %pad_maximum_fusion.1), channel_id=1, source_target_pairs={{0,1},{1,2},{2,3},{4,5},{5,6},{6,7},{8,9},{9,10},{10,11},{12,13},{... | collective-permute-start | bytes 49160 | tf_op jit(solution)/shard_map/ppermute | solution.py:500
  12.6 1.3 %collective-permute-start.3 = (bf16[2,8,2,256]{3,2,1,0:T(2,128)(2,1)S(1)}, bf16[2,8,2,256]{3,2,1,0:T(2,128)(2,1)S(1)}, u32[]{:S(2)}, u32[]{:S(2)}) collective-permute-start(bf16[2,8,2,256]{3,2,1,0:T(2,128)(2,1)S(1)} %pad_maximum_fusion.2), channel_id=1, source_target_pairs={{1,0},{2,1},{3,2},{5,4},{6,5},{7,6},{9,8},{10,9},{11,10},{13,12},{... | collective-permute-start | bytes 49160 | tf_op jit(solution)/shard_map/ppermute | solution.py:503
  14.3 1.0 copy.25
  16.6 0.8 collective-permute-done.3.right_hbm
  18.0 8.5 %window.3 = (f32[512,512]{1,0:T(8,128)}, bf16[8,4,2,8,512]{4,3,2,1,0:T(8,128)(2,1)}) custom-call(s32[4]{0:T(128)S(1)} %pad_add_fusion.place_ref, f32[2,8,64,512]{3,2,1,0:T(8,128)} %latent_hbm.3, bf16[2,4,32,256]{3,2,1,0:T(8,128)(2,1)} %context_hbm.3, bf16[2,2,32,256]{3,2,1,0:T(8,128)(2,1)} %copy-done.9, bf16[2,2,32,256]{3,2,1,0:T(8,128)(2,1)} %copy-done.8, ...), custom_call_target="tpu_custom_call" | custom-call | tf_op jit(solution)/shard_map/window/pallas_call | solution.py:444
  26.5 7.8 %all-to-all-start.2 = ((bf16[32,2,8,512]{3,2,1,0:T(8,128)(2,1)}), bf16[32,2,8,512]{3,2,1,0:T(8,128)(2,1)S(1)}, u32[]{:S(2)}, u32[]{:S(2)}) async-start(bf16[32,2,8,512]{3,2,1,0:T(8,128)(2,1)} %bitcast.29), calls=%async_computation.2 | async-start | bytes 1048576 | tf_op jit(solution)/shard_map/all_to_all | solution.py:628
  34.3 8.5 %window.2 = (f32[512,512]{1,0:T(8,128)}, bf16[8,4,2,8,512]{4,3,2,1,0:T(8,128)(2,1)}) custom-call(s32[4]{0:T(128)S(1)} %pad_add_fusion.place_ref, f32[2,8,64,512]{3,2,1,0:T(8,128)} %latent_hbm.3, bf16[2,4,32,256]{3,2,1,0:T(8,128)(2,1)} %context_hbm.3, bf16[2,2,32,256]{3,2,1,0:T(8,128)(2,1)} %copy-done.9, bf16[2,2,32,256]{3,2,1,0:T(8,128)(2,1)} %copy-done.8, ...), custom_call_target="tpu_custom_call" | custom-call | tf_op jit(solution)/shard_map/window/pallas_call | solution.py:444
  42.9 6.7 %all-to-all-done.2 = bf16[32,2,8,512]{3,2,1,0:T(8,128)(2,1)S(1)} async-done(((bf16[32,2,8,512]{3,2,1,0:T(8,128)(2,1)}), bf16[32,2,8,512]{3,2,1,0:T(8,128)(2,1)S(1)}, u32[]{:S(2)}, u32[]{:S(2)}) %all-to-all-start.2) | async-done | bytes 524320 | tf_op jit(solution)/shard_map/all_to_all | solution.py:628
  49.6 3.2 %all-to-all-start = ((bf16[32,2,8,512]{3,2,1,0:T(8,128)(2,1)}), bf16[32,2,8,512]{3,2,1,0:T(8,128)(2,1)S(1)}, u32[]{:S(2)}, u32[]{:S(2)}) async-start(bf16[32,2,8,512]{3,2,1,0:T(8,128)(2,1)} %bitcast.28), calls=%async_computation | async-start | bytes 1048576 | tf_op jit(solution)/shard_map/all_to_all | solution.py:628
  52.7 1.0 copy.26
  53.7 5.1 %grid.3 = bf16[512,512]{1,0:T(8,128)(2,1)} custom-call(bf16[512,512]{1,0:T(8,128)(2,1)} %bitcast.24, f32[64,1024]{1,0:T(8,128)} %copy-done.1, bf16[512,1536]{1,0:T(8,128)(2,1)} %qkv_hbm.7, bf16[512,512]{1,0:T(8,128)(2,1)} %bitcast.20), custom_call_target="tpu_custom_call" | custom-call | tf_op jit(solution)/shard_map/grid/pallas_call | solution.py:444
  58.9 9.1 %all-to-all-done = bf16[32,2,8,512]{3,2,1,0:T(8,128)(2,1)S(1)} async-done(((bf16[32,2,8,512]{3,2,1,0:T(8,128)(2,1)}), bf16[32,2,8,512]{3,2,1,0:T(8,128)(2,1)S(1)}, u32[]{:S(2)}, u32[]{:S(2)}) %all-to-all-start) | async-done | bytes 524320 | tf_op jit(solution)/shard_map/all_to_all | solution.py:628
  68.0 3.2 %all-to-all-start.3 = ((bf16[32,2,8,512]{3,2,1,0:T(8,128)(2,1)}), bf16[32,2,8,512]{3,2,1,0:T(8,128)(2,1)S(1)}, u32[]{:S(2)}, u32[]{:S(2)}) async-start(bf16[32,2,8,512]{3,2,1,0:T(8,128)(2,1)} %bitcast.27), calls=%async_computation.3 | async-start | bytes 1048576 | tf_op jit(solution)/shard_map/all_to_all | solution.py:636
  71.2 5.2 %grid.2 = bf16[512,512]{1,0:T(8,128)(2,1)} custom-call(bf16[512,512]{1,0:T(8,128)(2,1)} %bitcast.25, f32[64,1024]{1,0:T(8,128)} %copy-done.1, bf16[512,1536]{1,0:T(8,128)(2,1)} %qkv_hbm.7, bf16[512,512]{1,0:T(8,128)(2,1)} %bitcast.21), custom_call_target="tpu_custom_call" | custom-call | tf_op jit(solution)/shard_map/grid/pallas_call | solution.py:444
  76.3 10.1 %all-to-all-done.3 = bf16[32,2,8,512]{3,2,1,0:T(8,128)(2,1)S(1)} async-done(((bf16[32,2,8,512]{3,2,1,0:T(8,128)(2,1)}), bf16[32,2,8,512]{3,2,1,0:T(8,128)(2,1)S(1)}, u32[]{:S(2)}, u32[]{:S(2)}) %all-to-all-start.3) | async-done | bytes 524320 | tf_op jit(solution)/shard_map/all_to_all | solution.py:636
  86.4 3.2 %all-to-all-start.1 = ((bf16[32,2,8,512]{3,2,1,0:T(8,128)(2,1)}), bf16[32,2,8,512]{3,2,1,0:T(8,128)(2,1)S(1)}, u32[]{:S(2)}, u32[]{:S(2)}) async-start(bf16[32,2,8,512]{3,2,1,0:T(8,128)(2,1)} %bitcast.26), calls=%async_computation.1 | async-start | bytes 1048576 | tf_op jit(solution)/shard_map/all_to_all | solution.py:636
  89.6 6.5 %mlp.2.refs_6_ = f32[2,8,64,512]{3,2,1,0:T(8,128)} custom-call(f32[512,512]{1,0:T(8,128)} %get-tuple-element.15.refs_0_, bf16[8,4,2,8,512]{4,3,2,1,0:T(8,128)(2,1)} %bitcast.22, f32[1,512]{1,0:T(1,128)S(1)} %bitcast.14, bf16[512,512]{1,0:T(8,128)(2,1)} %refs_3_.3, bf16[512,2048]{1,0:T(8,128)(2,1)} %refs_4_.3, bf16[2048,512]{1,0:T(8,128)(2,1)} %refs_5_.3), custom_call_target="tpu_custom_call" | custom-call | tf_op jit(solution)/shard_map/mlp/pallas_call | solution.py:444
  96.1 8.8 %all-to-all-done.1 = bf16[32,2,8,512]{3,2,1,0:T(8,128)(2,1)S(1)} async-done(((bf16[32,2,8,512]{3,2,1,0:T(8,128)(2,1)}), bf16[32,2,8,512]{3,2,1,0:T(8,128)(2,1)S(1)}, u32[]{:S(2)}, u32[]{:S(2)}) %all-to-all-start.1) | async-done | bytes 524320 | tf_op jit(solution)/shard_map/all_to_all | solution.py:636
  104.8 0.8 copy-done.5
  105.6 6.5 %mlp.3 = f32[2,8,64,512]{3,2,1,0:T(8,128)} custom-call(f32[512,512]{1,0:T(8,128)} %get-tuple-element.12.refs_0_, bf16[8,4,2,8,512]{4,3,2,1,0:T(8,128)(2,1)} %bitcast.23, f32[1,512]{1,0:T(1,128)S(1)} %bitcast.15, bf16[512,512]{1,0:T(8,128)(2,1)} %refs_3_.3, bf16[512,2048]{1,0:T(8,128)(2,1)} %refs_4_.3, ...), custom_call_target="tpu_custom_call", output_to_operand_aliasing={{}: (6, {})} | custom-call | tf_op jit(solution)/shard_map/mlp/pallas_call | solution.py:444
  (39 shorter events, 3.2 us)
Async XLA Ops:
  0.0 15.3 %copy-start.2 = (bf16[8,225,128]{2,1,0:T(8,128)(2,1)S(1)}, bf16[8,225,128]{2,1,0:T(8,128)(2,1)}, u32[]{:S(2)}) copy-start(bf16[8,225,128]{2,1,0:T(8,128)(2,1)} %constant.25.clone.pick_ref) | copy-start | bytes 1382404
  0.0 14.2 %slice-start.1 = ((bf16[512,1536]{1,0:T(8,128)(2,1)}), bf16[512,512]{1,0:T(8,128)(2,1)S(1)}, s32[]{:S(2)}) async-start(bf16[512,1536]{1,0:T(8,128)(2,1)} %qkv_hbm.6), calls=%async_computation.5 | async-start | bytes 1048576 | tf_op jit(solution)/shard_map/slice | solution.py:519
  1.0 8.2 %collective-permute-start.1 = (bf16[2,2,32,256]{3,2,1,0:T(8,128)(2,1)S(1)}, bf16[2,2,32,256]{3,2,1,0:T(8,128)(2,1)S(1)}, u32[]{:S(2)}, u32[]{:S(2)}) collective-permute-start(bf16[2,2,32,256]{3,2,1,0:T(8,128)(2,1)S(1)} %get-tuple-element.19), channel_id=1, source_target_pairs={{4,0},{8,4},{12,8},{16,12},{20,16},{24,20},{28,24},{5,1},{9,5},{13... | collective-permute-start | bytes 196616 | tf_op jit(solution)/shard_map/ppermute | solution.py:27
  2.9 6.3 %collective-permute-start = (bf16[2,2,32,256]{3,2,1,0:T(8,128)(2,1)S(1)}, bf16[2,2,32,256]{3,2,1,0:T(8,128)(2,1)S(1)}, u32[]{:S(2)}, u32[]{:S(2)}) collective-permute-start(bf16[2,2,32,256]{3,2,1,0:T(8,128)(2,1)S(1)} %get-tuple-element.20), channel_id=1, source_target_pairs={{0,4},{4,8},{8,12},{12,16},{16,20},{20,24},{24,28},{1,5},{5,9},{9,... | collective-permute-start | bytes 196616 | tf_op jit(solution)/shard_map/ppermute | solution.py:24
  9.2 8.2 %copy-start.8 = (bf16[2,2,32,256]{3,2,1,0:T(8,128)(2,1)}, bf16[2,2,32,256]{3,2,1,0:T(8,128)(2,1)S(1)}, u32[]{:S(2)}) copy-start(bf16[2,2,32,256]{3,2,1,0:T(8,128)(2,1)S(1)} %collective-permute-done.1.high_hbm) | copy-start | bytes 196612
  9.3 8.1 %copy-start.9 = (bf16[2,2,32,256]{3,2,1,0:T(8,128)(2,1)}, bf16[2,2,32,256]{3,2,1,0:T(8,128)(2,1)S(1)}, u32[]{:S(2)}) copy-start(bf16[2,2,32,256]{3,2,1,0:T(8,128)(2,1)S(1)} %collective-permute-done.low_hbm) | copy-start | bytes 196612
  9.3 7.3 %collective-permute-start.2 = (bf16[2,8,2,256]{3,2,1,0:T(2,128)(2,1)S(1)}, bf16[2,8,2,256]{3,2,1,0:T(2,128)(2,1)S(1)}, u32[]{:S(2)}, u32[]{:S(2)}) collective-permute-start(bf16[2,8,2,256]{3,2,1,0:T(2,128)(2,1)S(1)} %pad_maximum_fusion.1), channel_id=1, source_target_pairs={{0,1},{1,2},{2,3},{4,5},{5,6},{6,7},{8,9},{9,10},{10,11},{12,13},{... | collective-permute-start | bytes 49160 | tf_op jit(solution)/shard_map/ppermute | solution.py:500
  12.6 4.8 %collective-permute-start.3 = (bf16[2,8,2,256]{3,2,1,0:T(2,128)(2,1)S(1)}, bf16[2,8,2,256]{3,2,1,0:T(2,128)(2,1)S(1)}, u32[]{:S(2)}, u32[]{:S(2)}) collective-permute-start(bf16[2,8,2,256]{3,2,1,0:T(2,128)(2,1)S(1)} %pad_maximum_fusion.2), channel_id=1, source_target_pairs={{1,0},{2,1},{3,2},{5,4},{6,5},{7,6},{9,8},{10,9},{11,10},{13,12},{... | collective-permute-start | bytes 49160 | tf_op jit(solution)/shard_map/ppermute | solution.py:503
  15.9 0.7 copy-start
  16.6 9.9 %copy-start.1 = (f32[64,1024]{1,0:T(8,128)}, f32[64,1024]{1,0:T(8,128)S(1)}, u32[]{:S(2)}) copy-start(f32[64,1024]{1,0:T(8,128)S(1)} %get-tuple-element.14.bias_hbm) | copy-start | bytes 786436
  16.6 0.8 copy-start.10
  17.4 0.6 copy-start.11
  26.5 23.0 %all-to-all-start.2 = ((bf16[32,2,8,512]{3,2,1,0:T(8,128)(2,1)}), bf16[32,2,8,512]{3,2,1,0:T(8,128)(2,1)S(1)}, u32[]{:S(2)}, u32[]{:S(2)}) async-start(bf16[32,2,8,512]{3,2,1,0:T(8,128)(2,1)} %bitcast.29), calls=%async_computation.2 | async-start | bytes 1048576 | tf_op jit(solution)/shard_map/all_to_all | solution.py:628
  42.8 9.9 %slice-start = ((bf16[512,1536]{1,0:T(8,128)(2,1)}), bf16[512,512]{1,0:T(8,128)(2,1)S(1)}, s32[]{:S(2)}) async-start(bf16[512,1536]{1,0:T(8,128)(2,1)} %qkv_hbm.7), calls=%async_computation.4 | async-start | bytes 1048576 | tf_op jit(solution)/shard_map/slice | solution.py:520
  49.6 4.2 %copy-start.6 = (bf16[32,2,8,512]{3,2,1,0:T(8,128)(2,1)}, bf16[32,2,8,512]{3,2,1,0:T(8,128)(2,1)S(1)}, u32[]{:S(2)}) copy-start(bf16[32,2,8,512]{3,2,1,0:T(8,128)(2,1)S(1)} %all-to-all-done.2) | copy-start | bytes 1572868
  49.6 18.4 %all-to-all-start = ((bf16[32,2,8,512]{3,2,1,0:T(8,128)(2,1)}), bf16[32,2,8,512]{3,2,1,0:T(8,128)(2,1)S(1)}, u32[]{:S(2)}, u32[]{:S(2)}) async-start(bf16[32,2,8,512]{3,2,1,0:T(8,128)(2,1)} %bitcast.28), calls=%async_computation | async-start | bytes 1048576 | tf_op jit(solution)/shard_map/all_to_all | solution.py:628
  68.0 3.2 %copy-start.7 = (bf16[32,2,8,512]{3,2,1,0:T(8,128)(2,1)}, bf16[32,2,8,512]{3,2,1,0:T(8,128)(2,1)S(1)}, u32[]{:S(2)}) copy-start(bf16[32,2,8,512]{3,2,1,0:T(8,128)(2,1)S(1)} %all-to-all-done) | copy-start | bytes 1572868
  68.0 18.4 %all-to-all-start.3 = ((bf16[32,2,8,512]{3,2,1,0:T(8,128)(2,1)}), bf16[32,2,8,512]{3,2,1,0:T(8,128)(2,1)S(1)}, u32[]{:S(2)}, u32[]{:S(2)}) async-start(bf16[32,2,8,512]{3,2,1,0:T(8,128)(2,1)} %bitcast.27), calls=%async_computation.3 | async-start | bytes 1048576 | tf_op jit(solution)/shard_map/all_to_all | solution.py:636
  71.2 18.4 %copy-start.3 = (f32[512]{0:T(512)S(1)}, f32[512]{0:T(512)}, u32[]{:S(2)}) copy-start(f32[512]{0:T(512)} %param.23) | copy-start | bytes 6148
  86.4 3.2 %copy-start.4 = (bf16[32,2,8,512]{3,2,1,0:T(8,128)(2,1)}, bf16[32,2,8,512]{3,2,1,0:T(8,128)(2,1)S(1)}, u32[]{:S(2)}) copy-start(bf16[32,2,8,512]{3,2,1,0:T(8,128)(2,1)S(1)} %all-to-all-done.3) | copy-start | bytes 1572868
  86.4 18.4 %all-to-all-start.1 = ((bf16[32,2,8,512]{3,2,1,0:T(8,128)(2,1)}), bf16[32,2,8,512]{3,2,1,0:T(8,128)(2,1)S(1)}, u32[]{:S(2)}, u32[]{:S(2)}) async-start(bf16[32,2,8,512]{3,2,1,0:T(8,128)(2,1)} %bitcast.26), calls=%async_computation.1 | async-start | bytes 1048576 | tf_op jit(solution)/shard_map/all_to_all | solution.py:636
  104.8 0.8 copy-start.5

commit v2 on v1

--- a/solution.py
+++ b/solution.py
@@ -13,22 +13,26 @@
 WIN = 8
 NORM_EPS = 1e-05
 LANES = 128
+HALVES = 2
 LOG2E = math.log2(math.e)
 JOINT = ("wide", "narrow")
 
 
-def neighbours(block, axis, dim, width):
+def neighbours(first, last, axis):
     count = lax.axis_size(axis)
-    forward = [(i, i + 1) for i in range(count - 1)]
-    backward = [(target, source) for source, target in forward]
-    low = lax.ppermute(
-        lax.slice_in_dim(block, block.shape[dim] - width, None, axis=dim), axis, forward
-    )
-    high = lax.ppermute(lax.slice_in_dim(block, 0, width, axis=dim), axis, backward)
-    return low, high
-
-
-def bias_kernel(flat_ref, pick_ref, window_ref, grid_ref, spread_s):
+    rounds = [
+        [pair for i in range(start, count - 1, 2) for pair in ((i, i + 1), (i + 1, i))]
+        for start in (0, 1)
+    ]
+    odd = lax.axis_index(axis) % 2 == 1
+    inner = lax.ppermute(jnp.where(odd, first, last), axis, rounds[0])
+    outer = lax.ppermute(jnp.where(odd, last, first), axis, rounds[1])
+    return jnp.where(odd, inner, outer), jnp.where(odd, outer, inner)
+
+
+def prepare_kernel(flat_ref, conv_hbm, window_ref, grid_ref, conv_ref, spread_s, sem):
+    conv_copy = pltpu.make_async_copy(conv_hbm, conv_ref, sem)
+    conv_copy.start()
     both, places = flat_ref.shape
     side = WIN
     flat = flat_ref[...] * LOG2E
@@ -37,8 +41,13 @@
     middle = rest.astype(jnp.bfloat16)
     last = (rest - middle.astype(jnp.float32)).astype(jnp.bfloat16)
     stacked = jnp.concatenate([top, middle, last], axis=0)
+    span = 2 * side - 1
+    place = lax.broadcasted_iota(jnp.int32, (places, LANES), 0)
+    lane = lax.broadcasted_iota(jnp.int32, (places, LANES), 1)
+    ahead = place - (lane // side) * span - lane % side - (side - 1)
     for key_col in range(side):
-        picked = jnp.dot(stacked, pick_ref[key_col], preferred_element_type=jnp.float32)
+        pick = jnp.where(ahead == -key_col, 1.0, 0.0).astype(jnp.bfloat16)
+        picked = jnp.dot(stacked, pick, preferred_element_type=jnp.float32)
         spread_s[pl.ds(key_col, both, stride=side), :] = (
             picked[:both] + picked[both : 2 * both]
         ) + picked[2 * both :]
@@ -56,17 +65,7 @@
                 table_ref[
                     key_row * side : (key_row + 1) * side, pair * LANES : (pair + 1) * LANES
                 ] = jnp.where(low_half, even_part, odd_part)
-
-
-def bias_pick(places):
-    side = WIN
-    span = 2 * side - 1
-    pick = np.zeros((side, places, LANES), np.float32)
-    for c in range(side):
-        for a in range(span):
-            for j in range(side):
-                pick[c, a * span + j + side - 1 - c, a * side + j] = 1.0
-    return jnp.asarray(pick, jnp.bfloat16)
+    conv_copy.wait()
 
 
 def layer_norm(values):
@@ -75,20 +74,20 @@
     return center * lax.rsqrt(spread + NORM_EPS)
 
 
-def project(normed_s, qk_w, vt_w, qk_s, vt_s, waits):
+def project(normed_s, qkv_w, qk_s, vt_s, wait):
     channels = normed_s.shape[1]
-    waits[0].wait()
+    wait.wait()
     queries = jnp.dot(
-        normed_s[...], qk_w[:, :channels], preferred_element_type=jnp.float32
+        normed_s[...], qkv_w[:, :channels], preferred_element_type=jnp.float32
     )
     qk_s[:, :channels] = (queries * (LOG2E * HEAD ** (-0.5))).astype(jnp.bfloat16)
     qk_s[:, channels:] = jnp.dot(
-        normed_s[...], qk_w[:, channels:], preferred_element_type=jnp.float32
+        normed_s[...], qkv_w[:, channels : 2 * channels], preferred_element_type=jnp.float32
     ).astype(jnp.bfloat16)
-    waits[1].wait()
-    values = lax.dot_general(
-        vt_w[...], normed_s[...], (((1,), (1,)), ((), ())), preferred_element_type=jnp.float32
-    ).astype(jnp.bfloat16)
+    values = jnp.dot(
+        normed_s[...], qkv_w[:, 2 * channels :], preferred_element_type=jnp.float32
+    )
+    values = values.T.astype(jnp.bfloat16)
     pairs, tall = vt_s.shape[:2]
     for pair in range(pairs):
         vt_s[pair, : 2 * HEAD] = values[pair * 2 * HEAD : (pair + 1) * 2 * HEAD]
@@ -166,31 +165,23 @@
 
 def window_kernel(
     place_ref,
+    low_ref,
+    high_ref,
+    left_ref,
+    right_ref,
+    bias_s,
+    conv_w,
+    context_hbm,
     latent_hbm,
-    context_hbm,
-    low_hbm,
-    high_hbm,
-    left_hbm,
-    right_hbm,
     lift_hbm,
-    bias_hbm,
-    conv_hbm,
     qkv_hbm,
-    vt_hbm,
     out_hbm,
     residual_hbm,
     normed_hbm,
     latent_ref,
     context_ref,
-    low_ref,
-    high_ref,
-    left_ref,
-    right_ref,
     lift_ref,
-    bias_s,
-    conv_w,
-    qk_w,
-    vt_w,
+    qkv_w,
     out_w,
     wide_s,
     taps_s,
@@ -214,47 +205,33 @@
     half_rows, half_cols, coarse = context_ref.shape
     members = WIN * WIN
     windows = cols // WIN
-    halo = [
-        pltpu.make_async_copy(source.at[sample], target, sems.at[0])
-        for source, target in (
-            (context_hbm, context_ref),
-            (low_hbm, low_ref),
-            (high_hbm, high_ref),
-            (left_hbm, left_ref),
-            (right_hbm, right_ref),
-        )
+    context_copy = pltpu.make_async_copy(context_hbm.at[sample], context_ref, sems.at[0])
+    cells_copies = [
+        pltpu.make_async_copy(lift_hbm, lift_ref, sems.at[1]),
+        pltpu.make_async_copy(latent_hbm.at[sample], latent_ref, sems.at[1]),
     ]
-    conv_copy = pltpu.make_async_copy(conv_hbm, conv_w, sems.at[1])
-    cells_copies = [
-        pltpu.make_async_copy(lift_hbm, lift_ref, sems.at[2]),
-        pltpu.make_async_copy(latent_hbm.at[sample], latent_ref, sems.at[2]),
-    ]
-    qk_copy = pltpu.make_async_copy(qkv_hbm.at[:, pl.ds(0, 2 * channels)], qk_w, sems.at[3])
-    vt_copy = pltpu.make_async_copy(vt_hbm, vt_w, sems.at[4])
-    bias_copy = pltpu.make_async_copy(bias_hbm, bias_s, sems.at[5])
-    placed = out_copies(out_hbm, out_w, sems.at[6])
-    for copy in halo + [conv_copy] + cells_copies + [qk_copy, vt_copy, bias_copy] + placed:
+    qkv_copy = pltpu.make_async_copy(qkv_hbm, qkv_w, sems.at[2])
+    placed = out_copies(out_hbm, out_w, sems.at[3])
+    for copy in [context_copy] + cells_copies + [qkv_copy] + placed:
         copy.start()
     span = half_rows + 2
-    for copy in halo:
-        copy.wait()
+    context_copy.wait()
     for row in range(half_rows + 4):
         base = row * stride
         if row < 2:
-            middle = low_ref[row]
+            middle = low_ref[sample, row]
         elif row < half_rows + 2:
             middle = context_ref[row - 2]
         else:
-            middle = high_ref[row - half_rows - 2]
-        wide_s[base + 6 : base + 8] = left_ref[row].astype(jnp.float32)
+            middle = high_ref[sample, row - half_rows - 2]
+        wide_s[base + 6 : base + 8] = left_ref[sample, row].astype(jnp.float32)
         wide_s[base + 8 : base + 8 + half_cols] = middle.astype(jnp.float32)
-        wide_s[base + 8 + half_cols : base + 10 + half_cols] = right_ref[row].astype(jnp.float32)
+        wide_s[base + 8 + half_cols : base + 10 + half_cols] = right_ref[sample, row].astype(jnp.float32)
     tall = (half_rows + 4) * stride
     for shift in range(3):
         taps_s[:, shift * coarse : (shift + 1) * coarse] = wide_s[
             shift + 6 : shift + 6 + tall
         ].astype(jnp.bfloat16)
-    conv_copy.wait()
     patches = jnp.concatenate(
         [taps_s[shift * stride : (shift + span) * stride] for shift in range(3)], axis=1
     )
@@ -280,8 +257,7 @@
         residual_ref[part] = residual
         normed_s[part] = layer_norm(residual).astype(jnp.bfloat16)
 
-    project(normed_s, qk_w, vt_w, qk_s, vt_s, (qk_copy, vt_copy))
-    bias_copy.wait()
+    project(normed_s, qkv_w, qk_s, vt_s, qkv_copy)
 
     def store_heads(window, heads):
         heads_s[window * members : (window + 1) * members] = heads.astype(jnp.bfloat16)
@@ -309,11 +285,9 @@
     cells_hbm,
     bias_hbm,
     qkv_hbm,
-    vt_hbm,
     heads_hbm,
     cells_ref,
-    qk_w,
-    vt_w,
+    qkv_w,
     spread_s,
     normed_s,
     qk_s,
@@ -329,9 +303,8 @@
     members = tokens // groups
     copies = [
         pltpu.make_async_copy(cells_hbm, cells_ref, sems.at[0]),
-        pltpu.make_async_copy(qkv_hbm.at[:, pl.ds(0, 2 * channels)], qk_w, sems.at[1]),
-        pltpu.make_async_copy(vt_hbm, vt_w, sems.at[2]),
-        pltpu.make_async_copy(bias_hbm, bias_s, sems.at[3]),
+        pltpu.make_async_copy(qkv_hbm, qkv_w, sems.at[1]),
+        pltpu.make_async_copy(bias_hbm, bias_s, sems.at[2]),
     ]
     for copy in copies:
         copy.start()
@@ -344,8 +317,8 @@
             normed_s[group * members : (group + 1) * members, lane] = spread_s[
                 chunk, pl.ds(group, members, stride=groups), :
             ].astype(jnp.bfloat16)
-    project(normed_s, qk_w, vt_w, qk_s, vt_s, copies[1:3])
-    copies[3].wait()
+    project(normed_s, qkv_w, qk_s, vt_s, copies[1])
+    copies[2].wait()
 
     def store_heads(group, heads):
         for chunk, lane in enumerate(lanes):
@@ -397,56 +370,58 @@
         pltpu.make_async_copy(first_hbm, first_w, sems.at[1]),
         pltpu.make_async_copy(second_hbm, second_w, sems.at[2]),
     ]
-    for copy in placed + cells + copies:
+    for copy in cells[:1] + placed + cells[1:] + copies:
         copy.start()
-    for copy in placed + cells:
-        copy.wait()
+    cells[0].wait()
     for window in range(windows):
         part = slice(window * members, (window + 1) * members)
         heads = heads_ref[:, window % narrow, window // narrow]
         normed_s[part] = heads.reshape(members, channels)
+    for copy in placed + cells[1:]:
+        copy.wait()
     residual_s[...] = residual_ref[...] + jnp.dot(
         normed_s[...], out_w[...], preferred_element_type=jnp.float32
     )
     for window in range(windows):
         part = slice(window * members, (window + 1) * members)
         normed_s[part] = (layer_norm(residual_s[part]) * gain_ref[...]).astype(jnp.bfloat16)
-    copies[0].wait()
-    for start in range(0, hidden, channels):
-        part = slice(start, start + channels)
-        inner = jnp.dot(normed_s[...], first_w[:, part], preferred_element_type=jnp.float32)
-        root = 0.7978845608028654
-        angle = inner * (root + (root * 0.044715) * (inner * inner))
-        halved = 0.5 * inner
-        active_s[:, part] = (halved + halved * jnp.tanh(angle)).astype(jnp.bfloat16)
-    copies[1].wait()
-    residual_s[...] += jnp.dot(active_s[...], second_w[...], preferred_element_type=jnp.float32)
+    for copy in copies:
+        copy.wait()
     stores = []
-    for window in range(windows):
-        store = pltpu.make_async_copy(
-            residual_s.at[pl.ds(window * members, members)].reshape(rows, WIN, channels),
-            result_hbm.at[sample, :, pl.ds(window * WIN, WIN), :],
-            sems.at[0],
-        )
-        store.start()
-        stores.append(store)
+    span = tokens // HALVES
+    for half in range(HALVES):
+        rows_in = slice(half * span, (half + 1) * span)
+        for start in range(0, hidden, channels):
+            part = slice(start, start + channels)
+            inner = jnp.dot(
+                normed_s[rows_in], first_w[:, part], preferred_element_type=jnp.float32
+            )
+            root = 0.7978845608028654
+            angle = inner * (root + (root * 0.044715) * (inner * inner))
+            active_s[half, :, part] = (inner * (1.0 + jnp.tanh(angle))).astype(jnp.bfloat16)
+        doubled = jnp.dot(active_s[half], second_w[...], preferred_element_type=jnp.float32)
+        residual_s[rows_in] = residual_s[rows_in] + 0.5 * doubled
+        for window in range(half * windows // HALVES, (half + 1) * windows // HALVES):
+            store = pltpu.make_async_copy(
+                residual_s.at[pl.ds(window * members, members)].reshape(rows, WIN, channels),
+                result_hbm.at[sample, :, pl.ds(window * WIN, WIN), :],
+                sems.at[0],
+            )
+            store.start()
+            stores.append(store)
     for store in stores:
         store.wait()
 
 
 VMEM = pl.BlockSpec(memory_space=pltpu.MemorySpace.VMEM)
+ANY = pl.BlockSpec(memory_space=pl.ANY)
 HBM = pl.BlockSpec(memory_space=pltpu.MemorySpace.HBM)
 SMEM = pl.BlockSpec(memory_space=pltpu.MemorySpace.SMEM)
 PARAMS = dict(vmem_limit_bytes=48 * 1024 * 1024)
 
 
-def pinned(call, *arrays):
-    return call(
-        *(
-            pltpu.with_memory_space_constraint(a, pltpu.HBM) if a.size > 1024 else a
-            for a in arrays
-        )
-    )
+def in_hbm(*arrays):
+    return [pltpu.with_memory_space_constraint(array, pltpu.HBM) for array in arrays]
 
 
 def lift_matrix(rows, cols, stride):
@@ -493,33 +468,31 @@
     assert windows == planes * narrow and WIN % split == 0
     stride = -(-(half_cols + 10) // 16) * 16
 
-    low, high = neighbours(context, "wide", 1, 2)
+    low, high = neighbours(context[:, :2], context[:, half_rows - 2 :], "wide")
     parts = (low, context, high)
-    forward = [(i, i + 1) for i in range(narrow - 1)]
-    backward = [(target, source) for source, target in forward]
-    left = lax.ppermute(
-        jnp.concatenate([part[:, :, half_cols - 2 :] for part in parts], axis=1), "narrow", forward
-    )
-    right = lax.ppermute(
-        jnp.concatenate([part[:, :, :2] for part in parts], axis=1), "narrow", backward
+    left, right = neighbours(
+        jnp.concatenate([part[:, :, :2] for part in parts], axis=1),
+        jnp.concatenate([part[:, :, half_cols - 2 :] for part in parts], axis=1),
+        "narrow",
     )
     heads_count = window_bias.shape[0]
     places = window_bias.shape[1] * window_bias.shape[2]
     flat_bias = jnp.concatenate([window_bias, grid_bias], axis=0).reshape(-1, places)
     table = jax.ShapeDtypeStruct((WIN * WIN, heads_count * WIN * WIN), jnp.float32)
-    window_table, grid_table = pl.pallas_call(
-        bias_kernel,
-        out_shape=(table, table),
-        in_specs=[VMEM, VMEM],
-        out_specs=(VMEM, VMEM),
-        scratch_shapes=[pltpu.VMEM((2 * heads_count * WIN, LANES), jnp.float32)],
+    conv_flat = conv_weight.reshape(9 * coarse, channels)
+    window_table, grid_table, conv_near = pl.pallas_call(
+        prepare_kernel,
+        out_shape=(table, table, jax.ShapeDtypeStruct(conv_flat.shape, conv_flat.dtype)),
+        in_specs=[VMEM, HBM],
+        out_specs=(VMEM, VMEM, VMEM),
+        scratch_shapes=[
+            pltpu.VMEM((2 * heads_count * WIN, LANES), jnp.float32),
+            pltpu.SemaphoreType.DMA,
+        ],
         compiler_params=pltpu.CompilerParams(**PARAMS),
-        name="bias",
-    )(flat_bias, bias_pick(places))
-    window_vt = window_qkv[:, 2 * channels :].T
-    grid_vt = grid_qkv[:, 2 * channels :].T
+        name="prepare",
+    )(flat_bias, *in_hbm(conv_flat))
     lift = lift_matrix(rows, cols, stride)
-    conv_flat = conv_weight.reshape(9 * coarse, channels)
     place = jnp.stack(
         [
             lax.axis_index("wide") * half_rows - 1,
@@ -539,20 +512,13 @@
                 pltpu.HBM((tokens, channels), f32),
                 pltpu.HBM((rows, narrow, planes, WIN, channels), bf16),
             ),
-            in_specs=[SMEM] + [HBM] * 12,
+            in_specs=[SMEM] + [VMEM] * 6 + [HBM] * 5,
             out_specs=(HBM, HBM),
             scratch_shapes=[
                 pltpu.VMEM((rows, cols, channels), f32),
                 pltpu.VMEM((half_rows, half_cols, coarse), bf16),
-                pltpu.VMEM((2, half_cols, coarse), bf16),
-                pltpu.VMEM((2, half_cols, coarse), bf16),
-                pltpu.VMEM((half_rows + 4, 2, coarse), bf16),
-                pltpu.VMEM((half_rows + 4, 2, coarse), bf16),
                 pltpu.VMEM((tokens, span * stride), bf16),
-                pltpu.VMEM((members, heads_count * members), f32),
-                pltpu.VMEM((9 * coarse, channels), bf16),
-                pltpu.VMEM((channels, 2 * channels), bf16),
-                pltpu.VMEM((channels, channels), bf16),
+                pltpu.VMEM((channels, 3 * channels), bf16),
                 pltpu.VMEM((channels, channels), bf16),
                 pltpu.VMEM(((half_rows + 4) * stride + 16, coarse), f32),
                 pltpu.VMEM(((half_rows + 4) * stride, 3 * coarse), bf16),
@@ -566,7 +532,7 @@
                 pltpu.VMEM((2, members, heads_count * members), bf16),
                 pltpu.VMEM((tokens, channels), bf16),
                 pltpu.VMEM((rows, narrow, planes, WIN, channels), bf16),
-                pltpu.SemaphoreType.DMA((7,)),
+                pltpu.SemaphoreType.DMA((4,)),
                 pltpu.SemaphoreType.DMA((2,)),
             ],
             compiler_params=pltpu.CompilerParams(**PARAMS),
@@ -576,12 +542,11 @@
     grid_call = pl.pallas_call(
         grid_kernel,
         out_shape=pltpu.HBM((tokens, channels), bf16),
-        in_specs=[HBM] * 4,
+        in_specs=[ANY] + [HBM] * 2,
         out_specs=HBM,
         scratch_shapes=[
             pltpu.VMEM((tokens, channels), bf16),
-            pltpu.VMEM((channels, 2 * channels), bf16),
-            pltpu.VMEM((channels, channels), bf16),
+            pltpu.VMEM((channels, 3 * channels), bf16),
             pltpu.VMEM((channels // LANES, tokens, LANES), f32),
             pltpu.VMEM((tokens, channels), bf16),
             pltpu.VMEM((tokens, 2 * channels), bf16),
@@ -590,7 +555,7 @@
             pltpu.VMEM((2, 1, heads_count * members), f32),
             pltpu.VMEM((2, members, heads_count * members), bf16),
             pltpu.VMEM((members, heads_count * members), f32),
-            pltpu.SemaphoreType.DMA((4,)),
+            pltpu.SemaphoreType.DMA((3,)),
         ],
         compiler_params=pltpu.CompilerParams(**PARAMS),
         name="grid",
@@ -601,7 +566,7 @@
         return pl.pallas_call(
             functools.partial(mlp_kernel, sample=sample),
             out_shape=pltpu.HBM((samples, rows, cols, channels), f32),
-            in_specs=[HBM, HBM, VMEM] + [HBM] * (3 if first else 4),
+            in_specs=[HBM, ANY, VMEM] + [HBM] * (3 if first else 4),
             out_specs=HBM,
             input_output_aliases={} if first else {6: 0},
             scratch_shapes=[
@@ -612,13 +577,19 @@
                 pltpu.VMEM((hidden, channels), bf16),
                 pltpu.VMEM((tokens, channels), f32),
                 pltpu.VMEM((tokens, channels), bf16),
-                pltpu.VMEM((tokens, hidden), bf16),
+                pltpu.VMEM((HALVES, tokens // HALVES, hidden), bf16),
                 pltpu.SemaphoreType.DMA((5,)),
             ],
             compiler_params=pltpu.CompilerParams(**PARAMS),
             name="mlp",
         )
 
+    context, latent, lift, window_qkv, window_out = in_hbm(
+        context, latent, lift, window_qkv, window_out
+    )
+    grid_table, grid_qkv, grid_out, mlp_in, mlp_out = in_hbm(
+        grid_table, grid_qkv, grid_out, mlp_in, mlp_out
+    )
     gain = mlp_gain.reshape(1, channels)
 
     def send(normed):
@@ -639,33 +610,31 @@
 
     residuals, cells = [], []
     for sample in range(samples):
-        residual, normed = pinned(
-            window_call(sample),
+        residual, normed = window_call(sample)(
             place,
-            latent,
-            context,
             low,
             high,
             left,
             right,
+            window_table,
+            conv_near,
+            context,
+            latent,
             lift,
-            window_table,
-            conv_flat,
             window_qkv,
-            window_vt,
             window_out,
         )
         residuals.append(residual)
         cells.append(send(normed))
     returned = []
     for sample in range(samples):
-        heads = pinned(grid_call, cells[sample], grid_table, grid_qkv, grid_vt)
+        heads = grid_call(cells[sample], grid_table, grid_qkv)
         returned.append(send_back(heads))
     result = ()
     for sample in range(samples):
         result = (
-            pinned(
-                mlp_call(sample), residuals[sample], returned[sample], gain, grid_out, mlp_in, mlp_out, *result
+            mlp_call(sample)(
+                residuals[sample], returned[sample], gain, grid_out, mlp_in, mlp_out, *result
             ),
         )
     return result[0]

time: 113 us -> 105 us (0.929)
  local copies, waits for them, and re-layouts: 6.21 us -> 1.12 us
  starting transfers between devices: 28.1 us -> 23.8 us
  waiting for transfers between devices: 35.4 us -> 37.4 us
  Pallas kernels: 40.9 us -> 39.3 us
    unnamed x26 -> x8, local copies, waits for them, and re-layouts: 4.13 us -> 0.02 us
    all_to_all x2, starting transfers between devices: 10.9 us -> 8.35 us  [send(): lax.all_to_all(pieces, JOINT, split_axis=0, concat_axis=0, tiled=True)]
    all_to_all x2, waiting for transfers between devices: 15.8 us -> 18 us  [send(): lax.all_to_all(pieces, JOINT, split_axis=0, concat_axis=0, tiled=True)]
    ppermute x4, starting transfers between devices: 10.9 us -> 9.14 us  [the longest x2 5.16 us: neighbours(): outer = lax.ppermute(jnp.where(odd, last, first), axis, rounds[1])]
    pallas_call x7, Pallas kernels: 40.9 us -> 39.3 us  [the longest x2 14.8 us: on_device(): window_call(sample)]
  transfers between devices with their start and end apart: 8 -> 8, of which waited for: 5 -> 4; matrix products, arithmetic and copies ran while one was open for 4% -> 2% of each run, Pallas kernels for 23% -> 25%
where the time goes in v2:
time: 105 us; the launch traced here: 104 us
  Pallas kernels  39.3 us (37%)
  waiting for transfers between devices  37.4 us (36%)
  starting transfers between devices  23.8 us (23%)
  other arithmetic  2.03 us (2%)
  local copies, waits for them, and re-layouts  1.12 us (1%)
    all_to_all x2, waiting for transfers between devices, send_back(): lax.all_to_all(pieces, JOINT, split_axis=0, concat_axis=0, tiled=True)  19.3 us
    all_to_all x2, waiting for transfers between devices, send(): lax.all_to_all(pieces, JOINT, split_axis=0, concat_axis=0, tiled=True)  18 us
    pallas_call x2, Pallas kernels, on_device(): window_call(sample)  14.8 us
    pallas_call x2, Pallas kernels, on_device(): mlp_call(sample)  12.1 us
    pallas_call x2, Pallas kernels, on_device(): heads = grid_call(cells[sample], grid_table, grid_qkv)  10.2 us
    all_to_all x2, starting transfers between devices, send(): lax.all_to_all(pieces, JOINT, split_axis=0, concat_axis=0, tiled=True)  8.35 us
    all_to_all x2, starting transfers between devices, send_back(): lax.all_to_all(pieces, JOINT, split_axis=0, concat_axis=0, tiled=True)  6.3 us
    ppermute x2, starting transfers between devices, neighbours(): outer = lax.ppermute(jnp.where(odd, last, first), axis, rounds[1])  5.16 us
  transfers between devices with their start and end apart: 8, of which 4 were waited for; matrix products, arithmetic and copies ran while one was open for 2% of the time, Pallas kernels for 25%

profile of v2, /device:TPU:1, one launch (start us, length us, event | category | flops | bytes accessed | tf_op | source)
XLA Modules:
  0.0 104.0 jit_solution(11631607996088807432)
XLA Ops:
  0.0 0.9 broadcast_select_fusion.2
  0.9 4.5 %collective-permute-start.1 = (bf16[2,2,32,256]{3,2,1,0:T(8,128)(2,1)S(1)}, bf16[2,2,32,256]{3,2,1,0:T(8,128)(2,1)S(1)}, u32[]{:S(2)}, u32[]{:S(2)}) collective-permute-start(bf16[2,2,32,256]{3,2,1,0:T(8,128)(2,1)S(1)} %get-tuple-element.23), channel_id=1, source_target_pairs={{4,8},{8,4},{12,16},{16,12},{20,24},{24,20},{5,9},{9,5},{13,17},{1... | collective-permute-start | bytes 196616 | tf_op jit(solution)/shard_map/ppermute | solution.py:29
  5.5 0.8 fusion
  6.3 1.0 pad_maximum_fusion
  7.4 0.7 collective-permute-start.3
  8.1 3.9 %collective-permute-start.2 = (bf16[2,8,2,256]{3,2,1,0:T(2,128)(2,1)S(1)}, bf16[2,8,2,256]{3,2,1,0:T(2,128)(2,1)S(1)}, u32[]{:S(2)}, u32[]{:S(2)}) collective-permute-start(bf16[2,8,2,256]{3,2,1,0:T(2,128)(2,1)S(1)} %get-tuple-element.32), channel_id=1, source_target_pairs={{0,1},{1,0},{2,3},{3,2},{4,5},{5,4},{6,7},{7,6},{8,9},{9,8},{10,11... | collective-permute-start | bytes 49160 | tf_op jit(solution)/shard_map/ppermute | solution.py:28
  12.0 0.1 pad_add_fusion.place_ref
  12.1 0.1 copy.18
  12.2 0.1 reshape.12.flat_ref
  12.4 2.2 %prepare.1 = (f32[64,1024]{1,0:T(8,128)S(1)}, f32[64,1024]{1,0:T(8,128)S(1)}, bf16[2304,512]{1,0:T(8,128)(2,1)S(1)}) custom-call(f32[32,225]{1,0:T(8,128)S(1)} %reshape.12.flat_ref, bf16[2304,512]{1,0:T(8,128)(2,1)} %bitcast.26), custom_call_target="tpu_custom_call" | custom-call | tf_op jit(solution)/shard_map/prepare/pallas_call | solution.py:483
  14.7 7.4 %window.3 = (f32[512,512]{1,0:T(8,128)}, bf16[8,4,2,8,512]{4,3,2,1,0:T(8,128)(2,1)}) custom-call(s32[4]{0:T(128)S(1)} %pad_add_fusion.place_ref, bf16[2,2,32,256]{3,2,1,0:T(8,128)(2,1)S(1)} %get-tuple-element.22.low_ref, bf16[2,2,32,256]{3,2,1,0:T(8,128)(2,1)S(1)} %get-tuple-element.21.high_ref, bf16[2,8,2,256]{3,2,1,0:T(2,128)(2,1)S(1)} %bitcast.22, ...), custom_call_target="tpu_custom_call" | custom-call | tf_op jit(solution)/shard_map/window/pallas_call | solution.py:613
  22.1 5.2 %all-to-all-start.2 = ((bf16[32,2,8,512]{3,2,1,0:T(8,128)(2,1)}), bf16[32,2,8,512]{3,2,1,0:T(8,128)(2,1)S(1)}, u32[]{:S(2)}, u32[]{:S(2)}) async-start(bf16[32,2,8,512]{3,2,1,0:T(8,128)(2,1)} %bitcast.30), calls=%async_computation.2 | async-start | bytes 1048576 | tf_op jit(solution)/shard_map/all_to_all | solution.py:599
  27.3 7.4 %window.2 = (f32[512,512]{1,0:T(8,128)}, bf16[8,4,2,8,512]{4,3,2,1,0:T(8,128)(2,1)}) custom-call(s32[4]{0:T(128)S(1)} %pad_add_fusion.place_ref, bf16[2,2,32,256]{3,2,1,0:T(8,128)(2,1)S(1)} %get-tuple-element.22.low_ref, bf16[2,2,32,256]{3,2,1,0:T(8,128)(2,1)S(1)} %get-tuple-element.21.high_ref, bf16[2,8,2,256]{3,2,1,0:T(2,128)(2,1)S(1)} %bitcast.23, ...), custom_call_target="tpu_custom_call" | custom-call | tf_op jit(solution)/shard_map/window/pallas_call | solution.py:613
  34.7 7.9 %all-to-all-done.2 = bf16[32,2,8,512]{3,2,1,0:T(8,128)(2,1)S(1)} async-done(((bf16[32,2,8,512]{3,2,1,0:T(8,128)(2,1)}), bf16[32,2,8,512]{3,2,1,0:T(8,128)(2,1)S(1)}, u32[]{:S(2)}, u32[]{:S(2)}) %all-to-all-start.2) | async-done | bytes 524320 | tf_op jit(solution)/shard_map/all_to_all | solution.py:599
  42.5 3.2 %all-to-all-start = ((bf16[32,2,8,512]{3,2,1,0:T(8,128)(2,1)}), bf16[32,2,8,512]{3,2,1,0:T(8,128)(2,1)S(1)}, u32[]{:S(2)}, u32[]{:S(2)}) async-start(bf16[32,2,8,512]{3,2,1,0:T(8,128)(2,1)} %bitcast.29), calls=%async_computation | async-start | bytes 1048576 | tf_op jit(solution)/shard_map/all_to_all | solution.py:599
  45.7 5.1 %grid.3 = bf16[512,512]{1,0:T(8,128)(2,1)} custom-call(bf16[512,512]{1,0:T(8,128)(2,1)S(1)} %bitcast.18, f32[64,1024]{1,0:T(8,128)} %copy-done.2, bf16[512,1536]{1,0:T(8,128)(2,1)} %qkv_hbm.7), custom_call_target="tpu_custom_call" | custom-call | tf_op jit(solution)/shard_map/grid/pallas_call | solution.py:631
  50.8 10.2 %all-to-all-done = bf16[32,2,8,512]{3,2,1,0:T(8,128)(2,1)S(1)} async-done(((bf16[32,2,8,512]{3,2,1,0:T(8,128)(2,1)}), bf16[32,2,8,512]{3,2,1,0:T(8,128)(2,1)S(1)}, u32[]{:S(2)}, u32[]{:S(2)}) %all-to-all-start) | async-done | bytes 524320 | tf_op jit(solution)/shard_map/all_to_all | solution.py:599
  61.0 3.2 %all-to-all-start.3 = ((bf16[32,2,8,512]{3,2,1,0:T(8,128)(2,1)}), bf16[32,2,8,512]{3,2,1,0:T(8,128)(2,1)S(1)}, u32[]{:S(2)}, u32[]{:S(2)}) async-start(bf16[32,2,8,512]{3,2,1,0:T(8,128)(2,1)} %bitcast.28), calls=%async_computation.3 | async-start | bytes 1048576 | tf_op jit(solution)/shard_map/all_to_all | solution.py:607
  64.1 5.1 %grid.2 = bf16[512,512]{1,0:T(8,128)(2,1)} custom-call(bf16[512,512]{1,0:T(8,128)(2,1)S(1)} %bitcast.19, f32[64,1024]{1,0:T(8,128)} %copy-done.2, bf16[512,1536]{1,0:T(8,128)(2,1)} %qkv_hbm.7), custom_call_target="tpu_custom_call" | custom-call | tf_op jit(solution)/shard_map/grid/pallas_call | solution.py:631
  69.3 10.1 %all-to-all-done.3 = bf16[32,2,8,512]{3,2,1,0:T(8,128)(2,1)S(1)} async-done(((bf16[32,2,8,512]{3,2,1,0:T(8,128)(2,1)}), bf16[32,2,8,512]{3,2,1,0:T(8,128)(2,1)S(1)}, u32[]{:S(2)}, u32[]{:S(2)}) %all-to-all-start.3) | async-done | bytes 524320 | tf_op jit(solution)/shard_map/all_to_all | solution.py:607
  79.4 3.2 %all-to-all-start.1 = ((bf16[32,2,8,512]{3,2,1,0:T(8,128)(2,1)}), bf16[32,2,8,512]{3,2,1,0:T(8,128)(2,1)S(1)}, u32[]{:S(2)}, u32[]{:S(2)}) async-start(bf16[32,2,8,512]{3,2,1,0:T(8,128)(2,1)} %bitcast.27), calls=%async_computation.1 | async-start | bytes 1048576 | tf_op jit(solution)/shard_map/all_to_all | solution.py:607
  82.6 6.1 %mlp.2.refs_6_ = f32[2,8,64,512]{3,2,1,0:T(8,128)} custom-call(f32[512,512]{1,0:T(8,128)S(1)} %copy-done, bf16[8,4,2,8,512]{4,3,2,1,0:T(8,128)(2,1)S(1)} %bitcast.16, f32[1,512]{1,0:T(1,128)S(1)} %bitcast.24, bf16[512,512]{1,0:T(8,128)(2,1)} %refs_3_.3, bf16[512,2048]{1,0:T(8,128)(2,1)} %refs_4_.3, bf16[2048,512]{1,0:T(8,128)(2,1)} %refs_5_.3), custom_call_target="tpu_custom_call" | custom-call | tf_op jit(solution)/shard_map/mlp/pallas_call | solution.py:636
  88.7 9.2 %all-to-all-done.1 = bf16[32,2,8,512]{3,2,1,0:T(8,128)(2,1)S(1)} async-done(((bf16[32,2,8,512]{3,2,1,0:T(8,128)(2,1)}), bf16[32,2,8,512]{3,2,1,0:T(8,128)(2,1)S(1)}, u32[]{:S(2)}, u32[]{:S(2)}) %all-to-all-start.1) | async-done | bytes 524320 | tf_op jit(solution)/shard_map/all_to_all | solution.py:607
  97.8 6.0 %mlp.3 = f32[2,8,64,512]{3,2,1,0:T(8,128)} custom-call(f32[512,512]{1,0:T(8,128)S(1)} %copy-done.1, bf16[8,4,2,8,512]{4,3,2,1,0:T(8,128)(2,1)S(1)} %bitcast.17, f32[1,512]{1,0:T(1,128)S(1)} %bitcast.25, bf16[512,512]{1,0:T(8,128)(2,1)} %refs_3_.3, bf16[512,2048]{1,0:T(8,128)(2,1)} %refs_4_.3, ...), custom_call_target="tpu_custom_call", output_to_operand_aliasing={{}: (6, {})} | custom-call | tf_op jit(solution)/shard_map/mlp/pallas_call | solution.py:636
  (17 shorter events, 0.2 us)
Async XLA Ops:
  0.9 6.4 %collective-permute-start.1 = (bf16[2,2,32,256]{3,2,1,0:T(8,128)(2,1)S(1)}, bf16[2,2,32,256]{3,2,1,0:T(8,128)(2,1)S(1)}, u32[]{:S(2)}, u32[]{:S(2)}) collective-permute-start(bf16[2,2,32,256]{3,2,1,0:T(8,128)(2,1)S(1)} %get-tuple-element.23), channel_id=1, source_target_pairs={{4,8},{8,4},{12,16},{16,12},{20,24},{24,20},{5,9},{9,5},{13,17},{1... | collective-permute-start | bytes 196616 | tf_op jit(solution)/shard_map/ppermute | solution.py:29
  5.4 1.9 %collective-permute-start = (bf16[2,2,32,256]{3,2,1,0:T(8,128)(2,1)S(1)}, bf16[2,2,32,256]{3,2,1,0:T(8,128)(2,1)S(1)}, u32[]{:S(2)}, u32[]{:S(2)}) collective-permute-start(bf16[2,2,32,256]{3,2,1,0:T(8,128)(2,1)S(1)} %get-tuple-element.24), channel_id=1, source_target_pairs={{0,4},{4,0},{8,12},{12,8},{16,20},{20,16},{24,28},{28,24},{1,5},{5... | collective-permute-start | bytes 196616 | tf_op jit(solution)/shard_map/ppermute | solution.py:28
  7.4 7.2 %collective-permute-start.3 = (bf16[2,8,2,256]{3,2,1,0:T(2,128)(2,1)S(1)}, bf16[2,8,2,256]{3,2,1,0:T(2,128)(2,1)S(1)}, u32[]{:S(2)}, u32[]{:S(2)}) collective-permute-start(bf16[2,8,2,256]{3,2,1,0:T(2,128)(2,1)S(1)} %get-tuple-element.31), channel_id=1, source_target_pairs={{1,2},{2,1},{5,6},{6,5},{9,10},{10,9},{13,14},{14,13},{17,18},{18,... | collective-permute-start | bytes 49160 | tf_op jit(solution)/shard_map/ppermute | solution.py:29
  8.1 6.5 %collective-permute-start.2 = (bf16[2,8,2,256]{3,2,1,0:T(2,128)(2,1)S(1)}, bf16[2,8,2,256]{3,2,1,0:T(2,128)(2,1)S(1)}, u32[]{:S(2)}, u32[]{:S(2)}) collective-permute-start(bf16[2,8,2,256]{3,2,1,0:T(2,128)(2,1)S(1)} %get-tuple-element.32), channel_id=1, source_target_pairs={{0,1},{1,0},{2,3},{3,2},{4,5},{5,4},{6,7},{7,6},{8,9},{9,8},{10,11... | collective-permute-start | bytes 49160 | tf_op jit(solution)/shard_map/ppermute | solution.py:28
  14.6 7.4 %copy-start.2 = (f32[64,1024]{1,0:T(8,128)}, f32[64,1024]{1,0:T(8,128)S(1)}, u32[]{:S(2)}) copy-start(f32[64,1024]{1,0:T(8,128)S(1)} %get-tuple-element.16.bias_hbm) | copy-start | bytes 786436
  22.1 20.5 %all-to-all-start.2 = ((bf16[32,2,8,512]{3,2,1,0:T(8,128)(2,1)}), bf16[32,2,8,512]{3,2,1,0:T(8,128)(2,1)S(1)}, u32[]{:S(2)}, u32[]{:S(2)}) async-start(bf16[32,2,8,512]{3,2,1,0:T(8,128)(2,1)} %bitcast.30), calls=%async_computation.2 | async-start | bytes 1048576 | tf_op jit(solution)/shard_map/all_to_all | solution.py:599
  42.5 18.4 %all-to-all-start = ((bf16[32,2,8,512]{3,2,1,0:T(8,128)(2,1)}), bf16[32,2,8,512]{3,2,1,0:T(8,128)(2,1)S(1)}, u32[]{:S(2)}, u32[]{:S(2)}) async-start(bf16[32,2,8,512]{3,2,1,0:T(8,128)(2,1)} %bitcast.29), calls=%async_computation | async-start | bytes 1048576 | tf_op jit(solution)/shard_map/all_to_all | solution.py:599
  61.0 18.4 %all-to-all-start.3 = ((bf16[32,2,8,512]{3,2,1,0:T(8,128)(2,1)}), bf16[32,2,8,512]{3,2,1,0:T(8,128)(2,1)S(1)}, u32[]{:S(2)}, u32[]{:S(2)}) async-start(bf16[32,2,8,512]{3,2,1,0:T(8,128)(2,1)} %bitcast.28), calls=%async_computation.3 | async-start | bytes 1048576 | tf_op jit(solution)/shard_map/all_to_all | solution.py:607
  64.1 18.4 %copy-start = (f32[512,512]{1,0:T(8,128)S(1)}, f32[512,512]{1,0:T(8,128)}, u32[]{:S(2)}) copy-start(f32[512,512]{1,0:T(8,128)} %get-tuple-element.17.refs_0_) | copy-start | bytes 3145732
  64.1 18.4 %copy-start.3 = (f32[512]{0:T(512)S(1)}, f32[512]{0:T(512)}, u32[]{:S(2)}) copy-start(f32[512]{0:T(512)} %param.22) | copy-start | bytes 6148
  79.4 18.4 %all-to-all-start.1 = ((bf16[32,2,8,512]{3,2,1,0:T(8,128)(2,1)}), bf16[32,2,8,512]{3,2,1,0:T(8,128)(2,1)S(1)}, u32[]{:S(2)}, u32[]{:S(2)}) async-start(bf16[32,2,8,512]{3,2,1,0:T(8,128)(2,1)} %bitcast.27), calls=%async_computation.1 | async-start | bytes 1048576 | tf_op jit(solution)/shard_map/all_to_all | solution.py:607
  82.6 15.2 %copy-start.1 = (f32[512,512]{1,0:T(8,128)S(1)}, f32[512,512]{1,0:T(8,128)}, u32[]{:S(2)}) copy-start(f32[512,512]{1,0:T(8,128)} %get-tuple-element.14.refs_0_) | copy-start | bytes 3145732
